TPU v7x, 32 devices: a whole 2x2x4 slice. The times are simulated.
32 devices in a mesh: band: 16 (over z, x, core), seq: 2 (over y).
Axes of the slice: x: 2, y: 2, z: 4, core: 2. Of those that a mesh axis runs over, the one named last changes fastest.
Arguments:
- tokens: bfloat16 [4, 1536, 1024], P('seq', 'band'), may hold values from -6 to 6
- segment_ids: int32 [4, 1536], P('seq'), may hold values from -1 to 2, as said below
- qkv_weight: bfloat16 [1024, 3072], P('seq'), may hold values from -0.1875 to 0.1875
- out_weight: bfloat16 [1024, 1024], P('seq'), may hold values from -3 to 3
- up_weight: bfloat16 [1024, 4096], P('seq'), may hold values from -0.1875 to 0.1875
- down_weight: bfloat16 [4096, 1024], P('seq'), may hold values from -0.09375 to 0.09375
- gain_first: bfloat16 [1024], P('seq'), may hold values from 0.5 to 1.5
- gain_second: bfloat16 [1024], P('seq'), may hold values from 0.5 to 1.5
- out_cotangent: bfloat16 [4, 1536, 1024], P('seq', 'band'), may hold values from -6 to 6
Outputs:
- layer_out: bfloat16 [4, 1536, 1024], P('seq', 'band')
- token_grad: float32 [4, 1536, 1024], P('seq', 'band')
- qkv_grad: float32 [1024, 3072], P('seq')
- outproj_grad: float32 [1024, 1024], P('seq')
- up_grad: float32 [1024, 4096], P('seq')
- down_grad: float32 [4096, 1024], P('seq')
- gain_first_grad: float32 [1024], P('seq')
- gain_second_grad: float32 [1024], P('seq')
Inputs may be any that keep to these rules, and one draw needn't show every extreme that they name: `segment_ids`: in each sequence the ids run 0, then 1, then 2, then -1 over four non-empty runs of positions, in that order; the run of 0 covers at least half, rounded down, of the positions that are not -1.
All inputs are finite; a program needn't handle non-finite values.
Results may differ from a plain program's by a relative error of at most 0.025.
Values may be sent and summed in bfloat16 or wider, within the bound.
A program may use at most 320 MiB of HBM per device.

v0:
```python
import math

import jax
import jax.numpy as jnp
from jax import lax
from jax.sharding import PartitionSpec as P

HEADS = 16
HEAD_DIM = 64


EPS = 1e-06
NEG = -1e30
ROOT_HALF = 0.7071067811865476
DENSITY = 0.3989422804014327


def layer_norm(values, gain):
    centre = values - jnp.mean(values, axis=-1, keepdims=True)
    inv_std = lax.rsqrt(jnp.mean(centre * centre, axis=-1, keepdims=True) + EPS)
    normed = centre * inv_std
    return (normed * gain, normed, inv_std)


def norm_back(grad_in, gain, normed, inv_std):
    scaled = grad_in * gain
    mean_one = jnp.mean(scaled, axis=-1, keepdims=True)
    mean_two = jnp.mean(scaled * normed, axis=-1, keepdims=True)
    gain_grad = jnp.sum((grad_in * normed).reshape(-1, grad_in.shape[-1]), axis=0)
    return (inv_std * (scaled - mean_one - normed * mean_two), gain_grad)


def split_heads(matrix):
    return matrix.reshape(matrix.shape[:-1] + (HEADS, HEAD_DIM))


def masked_scores(query_part, key_part, query_seg, key_seg):
    scores = jnp.einsum(
        "qhd,khd->hqk", query_part, key_part, preferred_element_type=jnp.float32
    ) * HEAD_DIM ** (-0.5)
    return (scores, (query_seg[:, None] == key_seg[None, :])[None])


def key_terms(
    query_part, dout_part, lse_part, delta_part, query_seg, key_part, value_part, key_seg
):
    scores, mask = masked_scores(query_part, key_part, query_seg, key_seg)
    probs = jnp.where(mask, jnp.exp(scores - lse_part[:, :, None]), 0.0)
    value_grad = jnp.einsum(
        "hqk,qhd->khd", probs.astype(jnp.bfloat16), dout_part, preferred_element_type=jnp.float32
    )
    prob_grad = jnp.einsum(
        "qhd,khd->hqk", dout_part, value_part, preferred_element_type=jnp.float32
    )
    score_grad = (probs * (prob_grad - delta_part[:, :, None])).astype(jnp.bfloat16)
    key_grad = jnp.einsum(
        "hqk,qhd->khd", score_grad, query_part, preferred_element_type=jnp.float32
    ) * HEAD_DIM ** (-0.5)
    return (key_grad, value_grad)


def online_step(query_part, query_seg):

    def step(state, item):
        key_block, value_block, seg_block = item
        run_max, run_sum, run_acc = state
        scores, mask = masked_scores(query_part, split_heads(key_block), query_seg, seg_block)
        masked = jnp.where(mask, scores, NEG)
        top = jnp.maximum(run_max, jnp.max(masked, axis=-1))
        correct = jnp.exp(run_max - top)
        probs = jnp.where(mask, jnp.exp(masked - top[:, :, None]), 0.0)
        update = jnp.einsum(
            "hqk,khd->hqd",
            probs.astype(jnp.bfloat16),
            split_heads(value_block),
            preferred_element_type=jnp.float32,
        )
        return (
            (
                top,
                run_sum * correct + jnp.sum(probs, axis=-1),
                run_acc * correct[:, :, None] + update,
            ),
            None,
        )

    return step


def per_device(
    tokens,
    segment_ids,
    qkv_weight,
    out_weight,
    up_weight,
    down_weight,
    gain_first,
    gain_second,
    out_cotangent,
):
    seqs_here = tokens.shape[0]
    tok_rows = tokens.shape[1]
    width = tokens.shape[2]
    my_seg = lax.dynamic_slice_in_dim(segment_ids, lax.axis_index("band") * tok_rows, tok_rows, 1)
    valid = (my_seg >= 0).astype(jnp.float32)[:, :, None]
    qkv_full, out_full, up_full, down_full, gain_one, gain_two = (
        lax.all_gather(qkv_weight, "seq", axis=0, tiled=True),
        lax.all_gather(out_weight, "seq", axis=0, tiled=True),
        lax.all_gather(up_weight, "seq", axis=0, tiled=True),
        lax.all_gather(down_weight, "seq", axis=0, tiled=True),
        lax.all_gather(gain_first, "seq", axis=0, tiled=True),
        lax.all_gather(gain_second, "seq", axis=0, tiled=True),
    )
    gain_one = gain_one.astype(jnp.float32)
    gain_two = gain_two.astype(jnp.float32)
    inputs = tokens.astype(jnp.float32)
    first_h, first_n, first_s = layer_norm(inputs, gain_one)
    first_low = first_h.astype(jnp.bfloat16)
    qkv_rows = jnp.einsum(
        "std,de->ste", first_low, qkv_full, preferred_element_type=jnp.float32
    ).astype(jnp.bfloat16)
    query_rows = qkv_rows[:, :, :width]
    key_rows = qkv_rows[:, :, width : 2 * width]
    value_rows = qkv_rows[:, :, 2 * width :]
    query_heads = split_heads(query_rows)

    def online(carry, pieces):
        key_piece, value_piece = pieces
        count = key_piece.shape[1]
        sub = math.gcd(count, 4 * tok_rows)
        results = []
        for member in range(seqs_here):
            state = (carry[0][member], carry[1][member], carry[2][member])
            stacked = (
                key_piece[member].reshape(count // sub, sub, width),
                value_piece[member].reshape(count // sub, sub, width),
                segment_ids[member].reshape(count // sub, sub),
            )
            state, _ = lax.scan(online_step(query_heads[member], my_seg[member]), state, stacked)
            results.append(state)
        return tuple((jnp.stack([result[part] for result in results]) for part in range(3)))

    start_state = (
        jnp.full((seqs_here, HEADS, tok_rows), NEG, jnp.float32),
        jnp.zeros((seqs_here, HEADS, tok_rows), jnp.float32),
        jnp.zeros((seqs_here, HEADS, tok_rows, HEAD_DIM), jnp.float32),
    )
    run_max, run_sum, run_acc = online(
        start_state,
        (
            lax.all_gather(key_rows, "band", axis=1, tiled=True),
            lax.all_gather(value_rows, "band", axis=1, tiled=True),
        ),
    )
    log_norm = run_max + jnp.log(run_sum)
    attn_heads = jnp.transpose(run_acc / run_sum[:, :, :, None], (0, 2, 1, 3))
    attn_rows = attn_heads.reshape(seqs_here, tok_rows, width)
    attn_low = attn_rows.astype(jnp.bfloat16)
    resid = inputs + valid * jnp.einsum(
        "std,de->ste", attn_low, out_full, preferred_element_type=jnp.float32
    )
    second_h, second_n, second_s = layer_norm(resid, gain_two)
    second_low = second_h.astype(jnp.bfloat16)
    pre_act = jnp.einsum("std,df->stf", second_low, up_full, preferred_element_type=jnp.float32)
    hidden_low = jax.nn.gelu(pre_act, approximate=False).astype(jnp.bfloat16)
    branch_two = jnp.einsum(
        "stf,fd->std", hidden_low, down_full, preferred_element_type=jnp.float32
    )
    layer_out = (resid + valid * branch_two).astype(jnp.bfloat16)
    grad_out = out_cotangent.astype(jnp.float32)
    grad_two = (valid * grad_out).astype(jnp.bfloat16)
    down_grad = jnp.einsum("stf,std->fd", hidden_low, grad_two, preferred_element_type=jnp.float32)
    hidden_grad = jnp.einsum("std,fd->stf", grad_two, down_full, preferred_element_type=jnp.float32)
    slope = 0.5 * (1.0 + lax.erf(pre_act * ROOT_HALF)) + pre_act * DENSITY * jnp.exp(
        -0.5 * pre_act * pre_act
    )
    pre_grad = (hidden_grad * slope).astype(jnp.bfloat16)
    up_grad = jnp.einsum("std,stf->df", second_low, pre_grad, preferred_element_type=jnp.float32)
    second_grad = jnp.einsum("stf,df->std", pre_grad, up_full, preferred_element_type=jnp.float32)
    norm_grad, gain_two_grad = norm_back(second_grad, gain_two, second_n, second_s)
    resid_grad = grad_out + norm_grad
    branch_grad = (valid * resid_grad).astype(jnp.bfloat16)
    outproj_grad = jnp.einsum(
        "std,ste->de", attn_low, branch_grad, preferred_element_type=jnp.float32
    )
    attn_grad = jnp.einsum(
        "ste,de->std", branch_grad, out_full, preferred_element_type=jnp.float32
    ).astype(jnp.bfloat16)
    dout_heads = split_heads(attn_grad)
    delta = jnp.transpose(jnp.sum(dout_heads.astype(jnp.float32) * attn_heads, axis=-1), (0, 2, 1))
    key_all, value_all = (
        lax.all_gather(key_rows, "band", axis=1, tiled=True),
        lax.all_gather(value_rows, "band", axis=1, tiled=True),
    )
    seq_len = key_all.shape[1]
    sub_all = math.gcd(seq_len, 4 * tok_rows)
    query_parts = []
    for member in range(seqs_here):
        blocks_all = (
            key_all[member].reshape(seq_len // sub_all, sub_all, width),
            value_all[member].reshape(seq_len // sub_all, sub_all, width),
            segment_ids[member].reshape(seq_len // sub_all, sub_all),
        )
        query_part = query_heads[member]
        dout_part = dout_heads[member]
        lse_part = log_norm[member]
        delta_part = delta[member]
        seg_part = my_seg[member]

        def query_step(
            total,
            item,
            query_part=query_part,
            dout_part=dout_part,
            lse_part=lse_part,
            delta_part=delta_part,
            seg_part=seg_part,
        ):
            key_block, value_block, seg_block = item
            scores, mask = masked_scores(query_part, split_heads(key_block), seg_part, seg_block)
            probs = jnp.where(mask, jnp.exp(scores - lse_part[:, :, None]), 0.0)
            prob_grad = jnp.einsum(
                "qhd,khd->hqk",
                dout_part,
                split_heads(value_block),
                preferred_element_type=jnp.float32,
            )
            score_grad = (probs * (prob_grad - delta_part[:, :, None])).astype(jnp.bfloat16)
            return (
                total
                + jnp.einsum(
                    "hqk,khd->qhd",
                    score_grad,
                    split_heads(key_block),
                    preferred_element_type=jnp.float32,
                ),
                None,
            )

        member_grad, _ = lax.scan(
            query_step, jnp.zeros((tok_rows, HEADS, HEAD_DIM), jnp.float32), blocks_all
        )
        query_parts.append(member_grad)
    query_grad = (jnp.stack(query_parts) * HEAD_DIM ** (-0.5)).reshape(seqs_here, tok_rows, width)
    count = lax.axis_size("band") * tok_rows
    sub = math.gcd(count, 4 * tok_rows)
    columns = []
    for member in range(seqs_here):
        key_part = key_all[member]
        value_part = value_all[member]
        seg_part = segment_ids[member]

        def one_block(item, member=member):
            key_block, value_block, seg_block = item
            key_grad, value_grad = key_terms(
                query_heads[member],
                dout_heads[member],
                log_norm[member],
                delta[member],
                my_seg[member],
                split_heads(key_block),
                split_heads(value_block),
                seg_block,
            )
            return jnp.concatenate(
                [key_grad.reshape(sub, width), value_grad.reshape(sub, width)], axis=-1
            )

        stacked = (
            key_part.reshape(count // sub, sub, width),
            value_part.reshape(count // sub, sub, width),
            seg_part.reshape(count // sub, sub),
        )
        columns.append(lax.map(one_block, stacked).reshape(count, 2 * width))
    both_grads = lax.psum_scatter(
        jnp.stack(columns, axis=1).astype(jnp.bfloat16), "band", scatter_dimension=0, tiled=True
    ).astype(jnp.float32)
    both_grads = jnp.transpose(both_grads, (1, 0, 2))
    key_grad = both_grads[:, :, :width]
    value_grad = both_grads[:, :, width:]
    qkv_grad_low = jnp.concatenate([query_grad, key_grad, value_grad], axis=-1).astype(jnp.bfloat16)
    qkv_grad = jnp.einsum(
        "std,ste->de", first_low, qkv_grad_low, preferred_element_type=jnp.float32
    )
    first_grad = jnp.einsum(
        "ste,de->std", qkv_grad_low, qkv_full, preferred_element_type=jnp.float32
    )
    in_grad, gain_one_grad = norm_back(first_grad, gain_one, first_n, first_s)
    token_grad = resid_grad + in_grad
    shares = (
        lax.psum_scatter(
            qkv_grad.astype(jnp.bfloat16), "seq", scatter_dimension=0, tiled=True
        ).astype(jnp.float32),
        lax.psum_scatter(
            outproj_grad.astype(jnp.bfloat16), "seq", scatter_dimension=0, tiled=True
        ).astype(jnp.float32),
        lax.psum_scatter(
            up_grad.astype(jnp.bfloat16), "seq", scatter_dimension=0, tiled=True
        ).astype(jnp.float32),
        lax.psum_scatter(
            down_grad.astype(jnp.bfloat16), "seq", scatter_dimension=0, tiled=True
        ).astype(jnp.float32),
        lax.psum_scatter(
            gain_one_grad.astype(jnp.bfloat16), "seq", scatter_dimension=0, tiled=True
        ).astype(jnp.float32),
        lax.psum_scatter(
            gain_two_grad.astype(jnp.bfloat16), "seq", scatter_dimension=0, tiled=True
        ).astype(jnp.float32),
    )
    summed = (
        lax.psum(shares[0].astype(jnp.bfloat16), "band").astype(jnp.float32),
        lax.psum(shares[1].astype(jnp.bfloat16), "band").astype(jnp.float32),
        lax.psum(shares[2].astype(jnp.bfloat16), "band").astype(jnp.float32),
        lax.psum(shares[3].astype(jnp.bfloat16), "band").astype(jnp.float32),
        lax.psum(shares[4].astype(jnp.bfloat16), "band").astype(jnp.float32),
        lax.psum(shares[5].astype(jnp.bfloat16), "band").astype(jnp.float32),
    )
    qkv_out, outproj_out, up_out, down_out, gain_one_out, gain_two_out = summed
    return (
        layer_out,
        token_grad,
        qkv_out,
        outproj_out,
        up_out,
        down_out,
        gain_one_out,
        gain_two_out,
    )


def solution(mesh):
    placed = (
        P("seq", "band", None),
        P("seq", None),
        P("seq", None),
        P("seq", None),
        P("seq", None),
        P("seq", None),
        P("seq"),
        P("seq"),
        P("seq", "band", None),
    )
    return jax.shard_map(
        per_device,
        mesh=mesh,
        in_specs=placed,
        out_specs=(
            P("seq", "band", None),
            P("seq", "band", None),
            P("seq", None),
            P("seq", None),
            P("seq", None),
            P("seq", None),
            P("seq"),
            P("seq"),
        ),
        check_vma=False,
    )
```

profile of v0, /device:TPU:0, one launch (start us, length us, event | category | flops | bytes accessed | tf_op | source)
XLA Modules:
  0.0 1317.6 jit_solution(2261456836373681363)
XLA Ops:
  8.0 5.3 all-gather
  13.7 79.0 %all-gather.9.cloned.1.call-done = bf16[1024,3072]{1,0:T(8,128)(2,1)} async-done(((bf16[512,3072]{1,0:T(8,128)(2,1)}), bf16[1024,3072]{1,0:T(8,128)(2,1)}) %all-gather.9.cloned.1.call-update) | async-done | bytes 6291472 | tf_op jit(solution)/shard_map/all_gather | solution.py:107
  107.3 52.6 %all-gather.13.cloned.1.call-done = bf16[2,1536,1024]{2,1,0:T(8,128)(2,1)} async-done(((bf16[2,96,1024]{2,1,0:T(8,128)(2,1)}), bf16[2,1536,1024]{2,1,0:T(8,128)(2,1)}) %all-gather.13.cloned.1.call-update) | async-done | bytes 6291472 | tf_op jit(solution)/shard_map/all_gather | solution.py:152
  160.0 5.2 fusion.186
  171.6 51.8 %all-gather.11.cloned.1.call-done = bf16[2,1536,1024]{2,1,0:T(8,128)(2,1)} async-done(((bf16[2,96,1024]{2,1,0:T(8,128)(2,1)}), bf16[2,1536,1024]{2,1,0:T(8,128)(2,1)}) %all-gather.11.cloned.1.call-update) | async-done | bytes 6291472 | tf_op jit(solution)/shard_map/all_gather | solution.py:151
  223.4 6.3 fusion.187
  239.1 19.7 %while.74 = (s32[]{:T(128)}, f32[16,96]{1,0:T(8,128)S(1)}, f32[16,96]{1,0:T(8,128)S(1)}, f32[16,96,64]{1,2,0:T(8,128)}, s32[1,96]{1,0:T(1,128)S(1)}, /*index=5*/...) while((s32[]{:T(128)}, f32[16,96]{1,0:T(8,128)S(1)}, ...), condition=%wide.region_5.6_spmd.clone, body=%wide.region_2.5_spmd.clone.sunk | while | flops 159002112 | bytes 16962652 | solution.py:139
  258.8 19.1 %while.75 = (s32[]{:T(128)}, f32[16,96]{1,0:T(8,128)S(1)}, f32[16,96]{1,0:T(8,128)S(1)}, f32[16,96,64]{1,2,0:T(8,128)}, s32[1,96]{1,0:T(1,128)S(1)}, /*index=5*/...) while((s32[]{:T(128)}, f32[16,96]{1,0:T(8,128)S(1)}, ...), condition=%wide.region_9.10_spmd.clone, body=%wide.region_6.9_spmd.clone.sunk | while | flops 159002112 | bytes 16176193 | solution.py:139
  283.7 78.3 %all-gather.17.cloned.1.call-done = bf16[1024,4096]{1,0:T(8,128)(2,1)} async-done(((bf16[512,4096]{1,0:T(8,128)(2,1)}), bf16[1024,4096]{1,0:T(8,128)(2,1)}) %all-gather.17.cloned.1.call-update) | async-done | bytes 8388624 | tf_op jit(solution)/shard_map/all_gather | solution.py:109
  362.0 9.1 fusion.178
  371.1 96.3 %all-gather.19.cloned.1.call-done = bf16[4096,1024]{1,0:T(8,128)(2,1)} async-done(((bf16[2048,1024]{1,0:T(8,128)(2,1)}), bf16[4096,1024]{1,0:T(8,128)(2,1)}) %all-gather.19.cloned.1.call-update) | async-done | bytes 8388624 | tf_op jit(solution)/shard_map/all_gather | solution.py:110
  467.4 6.7 fusion.121
  488.0 48.8 %while.73 = (s32[]{:T(128)}, bf16[4,384,2048]{1,2,0:T(8,128)(2,1)}, s32[2,96]{1,0:T(2,128)S(1)}, s32[4,384]{1,0:T(4,128)S(1)}, bf16[4,384,1024]{1,2,0:T(8,128)(2...) while((s32[]{:T(128)}, bf16[4,384,2048]{1,2,0:T(8,128)(2,1)}, ...), condition=%wide.region_22.23_spmd, body=%wide.region_21.22_spmd.sunk | while | flops 311857152 | bytes 22441784 | solution.py:274
  536.9 9.0 copy.88
  549.1 33.9 %while.72 = (s32[]{:T(128)}, bf16[4,384,2048]{1,2,0:T(8,128)(2,1)}, s32[2,96]{1,0:T(2,128)S(1)}, s32[4,384]{1,0:T(4,128)S(1)}, bf16[4,384,1024]{1,2,0:T(8,128)(2...) while((s32[]{:T(128)}, bf16[4,384,2048]{1,2,0:T(8,128)(2,1)}, ...), condition=%wide.region_20.21_spmd, body=%wide.region_19.20_spmd.sunk | while | flops 311857152 | bytes 19296028 | solution.py:274
  582.9 9.0 copy.85
  591.9 10.5 pad_maximum_fusion
  607.2 6.7 bitcast_convert_fusion.1
  616.2 8.2 fusion.129
  625.5 5.8 bitcast_convert_fusion
  633.9 26.6 %while.76 = (s32[]{:T(128)}, f32[96,16,64]{0,2,1:T(8,128)}, bf16[4,384,1024]{1,2,0:T(8,128)(2,1)}, s32[1,96]{1,0:T(1,128)S(1)}, s32[4,384]{1,0:T(4,128)S(1)}, /*...) while((s32[]{:T(128)}, f32[96,16,64]{0,2,1:T(8,128)}, ...), condition=%wide.region_16.17_spmd.clone, body=%wide.region_15.16_spmd.clone.sunk | while | flops 230264832 | bytes 12280875 | solution.py:240
  664.3 26.4 %while.77 = (s32[]{:T(128)}, f32[96,16,64]{0,2,1:T(8,128)}, bf16[4,384,1024]{1,2,0:T(8,128)(2,1)}, s32[1,96]{1,0:T(1,128)S(1)}, s32[4,384]{1,0:T(4,128)S(1)}, /*...) while((s32[]{:T(128)}, f32[96,16,64]{0,2,1:T(8,128)}, ...), condition=%wide.region_18.19_spmd.clone, body=%wide.region_17.18_spmd.clone.sunk | while | flops 230264832 | bytes 11494415 | solution.py:240
  693.0 44.3 %reduce-scatter.6.cloned.1.call-done = bf16[96,2,2048]{2,0,1:T(8,128)(2,1)} async-done(((bf16[1536,2,2048]{2,0,1:T(8,128)(2,1)}), bf16[96,2,2048]{2,0,1:T(8,128)(2,1)}) %reduce-scatter.6.cloned.1.call-update) | async-done | bytes 786448 | tf_op jit(solution)/shard_map/reduce_scatter | solution.py:275
  737.4 5.9 bitcast_convert_fusion.2
  743.3 27.8 %reduce-scatter.10.cloned.1.call-done = bf16[512,1024]{1,0:T(8,128)(2,1)} async-done(((bf16[1024,1024]{1,0:T(8,128)(2,1)}), bf16[512,1024]{1,0:T(8,128)(2,1)}) %reduce-scatter.10.cloned.1.call-update) | async-done | bytes 1048592 | tf_op jit(solution)/shard_map/reduce_scatter | solution.py:294
  771.2 102.2 %reduce-scatter.12.cloned.1.call-done = bf16[512,4096]{1,0:T(8,128)(2,1)} async-done(((bf16[1024,4096]{1,0:T(8,128)(2,1)}), bf16[512,4096]{1,0:T(8,128)(2,1)}) %reduce-scatter.12.cloned.1.call-update) | async-done | bytes 4194320 | tf_op jit(solution)/shard_map/reduce_scatter | solution.py:297
  873.4 102.0 %reduce-scatter.14.cloned.1.call-done = bf16[2048,1024]{1,0:T(8,128)(2,1)} async-done(((bf16[4096,1024]{1,0:T(8,128)(2,1)}), bf16[2048,1024]{1,0:T(8,128)(2,1)}) %reduce-scatter.14.cloned.1.call-update) | async-done | bytes 4194320 | tf_op jit(solution)/shard_map/reduce_scatter | solution.py:300
  975.4 80.1 %reduce-scatter.8.cloned.1.call-done = bf16[512,3072]{1,0:T(8,128)(2,1)} async-done(((bf16[1024,3072]{1,0:T(8,128)(2,1)}), bf16[512,3072]{1,0:T(8,128)(2,1)}) %reduce-scatter.8.cloned.1.call-update) | async-done | bytes 3145744 | tf_op jit(solution)/shard_map/reduce_scatter | solution.py:291
  1057.4 6.0 fusion.158
  1063.4 6.0 fusion.173
  1074.6 34.1 %all-reduce.2 = (bf16[512]{0:T(512)(128)(2,1)S(1)}, bf16[512]{0:T(512)(128)(2,1)S(1)}) all-reduce(bf16[512]{0:T(512)(128)(2,1)S(1)} %dynamic-slice.1, bf16[512]{0:T(512)(128)(2,1)S(1)} %dynamic-slice.3), channel_id=1, replica_groups=mesh['band'=16,'seq'=2] {'band'}, use_global_device_ids=true, to_apply=%region_36.37 | all-reduce | flops 1024 | bytes 4096 | tf_op jit(solution)/shard_map/psum | solution.py:315
  1111.0 184.1 %all-reduce.7.cloned.1.call-done = (bf16[512,3072]{1,0:T(8,128)(2,1)}, bf16[512,1024]{1,0:T(8,128)(2,1)}, bf16[512,4096]{1,0:T(8,128)(2,1)}, bf16[2048,1024]{1,0:T(8,128)(2,1)}) async-done(((bf16[512,3072]{1,0:T(8,128)(2,1)}, bf16[512,1024]{1,0:T(8,128)(2,1)}, bf16[512,4096]{1,0:T(8,128)(2,1)}, bf16[2048,1024]{1,0:T(8,128)(2,1)}), (bf16[512,3072]{1,0:T(8,128)(2,1)}, bf16[512,1024]{1,0:T(8,128)(2,1)}, ...) | async-done | bytes 12582928 | tf_op jit(solution)/shard_map/psum | solution.py:311
  (419 shorter events, 268.7 us)
Async XLA Ops:
  7.2 6.1 copy-start.13
  7.2 85.5 %all-gather.9.cloned.1.call-start = ((), (), s32[]{:S(2)}) async-start(), calls=%async_computation.5 | async-start | bytes 9437184 | tf_op jit(solution)/shard_map/all_gather | solution.py:107
  7.9 152.0 %all-gather.13.cloned.1.call-start = ((), (), s32[]{:S(2)}) async-start(), calls=%async_computation.7 | async-start | bytes 6684672 | tf_op jit(solution)/shard_map/all_gather | solution.py:152
  13.3 83.7 %copy-start.33 = (f32[2,1,512]{2,1,0:T(1,128)}, f32[2,1,512]{2,1,0:T(1,128)S(1)}, u32[]{:S(2)}) copy-start(f32[2,1,512]{2,1,0:T(1,128)S(1)} %convert_element_type.155) | copy-start | bytes 12292
  13.4 83.5 %copy-start.35 = (f32[2,96]{1,0:T(2,128)}, f32[2,96]{1,0:T(2,128)S(1)}, u32[]{:S(2)}) copy-start(f32[2,96]{1,0:T(2,128)S(1)} %broadcast_multiply_fusion.5) | copy-start | bytes 2308
  13.7 83.3 %copy-start.37 = (f32[2,96]{1,0:T(2,128)}, f32[2,96]{1,0:T(2,128)S(1)}, u32[]{:S(2)}) copy-start(f32[2,96]{1,0:T(2,128)S(1)} %add_rsqrt_fusion.1) | copy-start | bytes 2308
  98.0 125.4 %all-gather.11.cloned.1.call-start = ((), (), s32[]{:S(2)}) async-start(), calls=%async_computation.6 | async-start | bytes 6684672 | tf_op jit(solution)/shard_map/all_gather | solution.py:151
  98.7 181.4 %all-gather.15.cloned.1.call-start = ((), (), s32[]{:S(2)}) async-start(), calls=%async_computation.8 | async-start | bytes 3145728 | tf_op jit(solution)/shard_map/all_gather | solution.py:108
  99.3 262.7 %all-gather.17.cloned.1.call-start = ((), (), s32[]{:S(2)}) async-start(), calls=%async_computation.9 | async-start | bytes 12582912 | tf_op jit(solution)/shard_map/all_gather | solution.py:109
  99.9 367.5 %all-gather.19.cloned.1.call-start = ((), (), s32[]{:S(2)}) async-start(), calls=%async_computation.10 | async-start | bytes 12582912 | tf_op jit(solution)/shard_map/all_gather | solution.py:110
  100.5 636.9 %reduce-scatter.6.cloned.1.call-start = ((), (), s32[]{:S(2)}) async-start(), calls=%async_computation.11 | async-start | bytes 13369344 | tf_op jit(solution)/shard_map/reduce_scatter | solution.py:275
  467.4 6.7 copy-start.7
  467.4 7.1 copy-start.42
  474.5 3.1 copy-start.30
  474.5 3.1 copy-start.28
  536.8 9.0 copy-start
  602.4 3.4 copy-start.8
  602.4 168.7 %reduce-scatter.10.cloned.1.call-start = ((), (), s32[]{:S(2)}) async-start(), calls=%async_computation.13 | async-start | bytes 3145728 | tf_op jit(solution)/shard_map/reduce_scatter | solution.py:294
  605.8 267.6 %reduce-scatter.12.cloned.1.call-start = ((), (), s32[]{:S(2)}) async-start(), calls=%async_computation.14 | async-start | bytes 12582912 | tf_op jit(solution)/shard_map/reduce_scatter | solution.py:297
  613.9 361.5 %reduce-scatter.14.cloned.1.call-start = ((), (), s32[]{:S(2)}) async-start(), calls=%async_computation.15 | async-start | bytes 12582912 | tf_op jit(solution)/shard_map/reduce_scatter | solution.py:300
  613.9 11.6 copy-start.29
  631.4 424.1 %reduce-scatter.8.cloned.1.call-start = ((), (), s32[]{:S(2)}) async-start(), calls=%async_computation.12 | async-start | bytes 9437184 | tf_op jit(solution)/shard_map/reduce_scatter | solution.py:291
  664.3 73.1 %copy-start.34 = (f32[2,1,512]{2,1,0:T(1,128)S(1)}, f32[2,1,512]{2,1,0:T(1,128)}, u32[]{:S(2)}) copy-start(f32[2,1,512]{2,1,0:T(1,128)} %copy-done.33) | copy-start | bytes 12292
  664.3 73.1 %copy-start.36 = (f32[2,96]{1,0:T(2,128)S(1)}, f32[2,96]{1,0:T(2,128)}, u32[]{:S(2)}) copy-start(f32[2,96]{1,0:T(2,128)} %copy-done.35) | copy-start | bytes 2308
  664.3 73.1 %copy-start.38 = (f32[2,96]{1,0:T(2,128)S(1)}, f32[2,96]{1,0:T(2,128)}, u32[]{:S(2)}) copy-start(f32[2,96]{1,0:T(2,128)} %copy-done.37) | copy-start | bytes 2308
  743.3 551.8 %all-reduce.7.cloned.1.call-start = ((), (), s32[]{:S(2)}) async-start(), calls=%async_computation.16 | async-start | bytes 25165824 | tf_op jit(solution)/shard_map/psum | solution.py:311
  1057.4 6.0 copy-start.14
  1057.4 6.0 copy-start.32
  1063.4 46.4 %copy-start.12 = (f32[2,96,1024]{2,1,0:T(8,128)S(1)}, f32[2,96,1024]{2,1,0:T(8,128)}, u32[]{:S(2)}) copy-start(f32[2,96,1024]{2,1,0:T(8,128)} %copy-done.10) | copy-start | bytes 2359300
  1295.1 2.9 copy-start.23
  1298.1 3.5 copy-start.20
  1301.6 4.5 copy-start.19
  (51 other events, 83.9 us)
Sparse Core Ops, SparseCore 0:
  9.6 83.0 all-gather.8
  98.1 61.8 all-gather.12
  162.8 60.5 all-gather.10
  224.8 31.6 all-gather.14
  257.9 103.9 all-gather.16
  363.4 104.0 all-gather.18
  602.6 134.7 reduce-scatter.5
  740.2 30.9 reduce-scatter.9
  774.2 99.2 reduce-scatter.11
  876.1 99.2 reduce-scatter.13
  978.4 77.0 reduce-scatter.7
  1059.9 235.1 all-reduce.6
where the time goes:
time: 1320 us
  waiting for transfers between devices  902 us (68%)
  matrix products  157 us (12%)
  local copies, waits for them, and re-layouts  131 us (10%)
  other arithmetic  61.8 us (5%)
  blocking collectives  48.8 us (4%)
  between operations  15.5 us (1%)
    psum x1, waiting for transfers between devices, per_device(): lax.psum(shares[0].astype(jnp.bfloat16), 'band').astype(jnp.float32)  184 us
    reduce_scatter x1, waiting for transfers between devices, per_device(): lax.psum_scatter(up_grad.astype(jnp.bfloat16), 'seq', scatter_dimension=0...  102 us
    reduce_scatter x1, waiting for transfers between devices, per_device(): lax.psum_scatter(down_grad.astype(jnp.bfloat16), 'seq', scatter_dimension...  102 us
    all_gather x1, waiting for transfers between devices, per_device(): lax.all_gather(down_weight, 'seq', axis=0, tiled=True)  96.3 us
    reduce_scatter x1, waiting for transfers between devices, per_device(): lax.psum_scatter(qkv_grad.astype(jnp.bfloat16), 'seq', scatter_dimension=...  80.1 us
    all_gather x1, waiting for transfers between devices, per_device(): lax.all_gather(qkv_weight, 'seq', axis=0, tiled=True)  79 us
    all_gather x1, waiting for transfers between devices, per_device(): lax.all_gather(up_weight, 'seq', axis=0, tiled=True)  78.3 us
    all_gather x1, waiting for transfers between devices, per_device(): lax.all_gather(value_rows, 'band', axis=1, tiled=True)  52.6 us
  transfers between devices with their start and end apart: 12, of which 11 were waited for; matrix products, arithmetic and copies ran while one was open for 14% of the time, Pallas kernels for 0%

commit v1 on v0

--- a/solution.py
+++ b/solution.py
@@ -1,8 +1,11 @@
+import functools
 import math
 
 import jax
 import jax.numpy as jnp
 from jax import lax
+from jax.experimental import pallas as pl
+from jax.experimental.pallas import tpu as pltpu
 from jax.sharding import PartitionSpec as P
 
 HEADS = 16
@@ -328,6 +331,624 @@
     )
 
 
+MESH = pl.DeviceIdType.MESH
+BF = jnp.bfloat16
+F32 = jnp.float32
+SCALE = HEAD_DIM ** (-0.5)
+
+
+def place():
+    b = lax.axis_index("band")
+    y = lax.axis_index("seq")
+    return b, y, b // 4, (b // 2) % 2, b % 2
+
+
+def meet(peers):
+    sem = pltpu.get_barrier_semaphore()
+    for peer in peers:
+        pl.semaphore_signal(sem, inc=1, device_id=peer, device_id_type=MESH)
+    pl.semaphore_wait(sem, len(peers))
+
+
+def send(src, dst, ssem, rsem, peer):
+    copy = pltpu.make_async_remote_copy(
+        src_ref=src, dst_ref=dst, send_sem=ssem, recv_sem=rsem, device_id=peer, device_id_type=MESH
+    )
+    copy.start()
+    return copy
+
+
+def comm_call(body, name, cid, outs, scratch, n_in):
+    vm = pl.BlockSpec(memory_space=pltpu.VMEM)
+    return pl.pallas_call(
+        body,
+        out_shape=[jax.ShapeDtypeStruct(s, d) for s, d in outs],
+        in_specs=[vm] * n_in,
+        out_specs=[vm] * len(outs),
+        scratch_shapes=scratch,
+        compiler_params=pltpu.CompilerParams(collective_id=cid, has_side_effects=True),
+        name=name,
+    )
+
+
+def dma(n):
+    return pltpu.SemaphoreType.DMA((n,))
+
+
+def norm_rows(v):
+    centre = v - jnp.mean(v, axis=-1, keepdims=True)
+    inv_std = lax.rsqrt(jnp.mean(centre * centre, axis=-1, keepdims=True) + EPS)
+    return centre * inv_std, inv_std
+
+
+def open_body(tok, seg, wqkv, gains, tok_all, seg_all, w_sel, gains_all, ss, rs):
+    b, y, z, x, c = place()
+    core, over = (b + 1 - 2 * c, y), (b, 1 - y)
+    meet([core, over])
+    cps = []
+    for m in range(2):
+        cps.append(send(tok.at[m], tok_all.at[2 * y + m, c], ss.at[m], rs.at[m], over))
+    cps.append(send(seg, seg_all.at[y], ss.at[2], rs.at[2], over))
+    cps.append(send(gains, gains_all.at[y], ss.at[3], rs.at[3], over))
+    k = 4
+    far = (1 - y) * 2 + c
+    own = y * 2 + c
+    for hp in range(2):
+        for p in range(3):
+            col = pl.multiple_of(p * 1024 + far * 256 + hp * 128, 128)
+            dst = w_sel.at[y, :, pl.ds(hp * 384 + p * 128, 128)]
+            cps.append(send(wqkv.at[:, pl.ds(col, 128)], dst, ss.at[k], rs.at[k], over))
+            k += 1
+    side = []
+    for m in range(2):
+        side.append(send(tok.at[m], tok_all.at[2 * y + m, c], ss.at[k], rs.at[k], core))
+        k += 1
+    for hp in range(2):
+        for p in range(3):
+            col = pl.multiple_of(p * 1024 + own * 256 + hp * 128, 128)
+            w_sel[y, :, hp * 384 + p * 128 : hp * 384 + p * 128 + 128] = wqkv[:, pl.ds(col, 128)]
+    for m in range(2):
+        tok_all[2 * y + m, c] = tok[m]
+    seg_all[y] = seg[...]
+    gains_all[y] = gains[...]
+    for m in range(2):
+        cps[m].wait_recv()
+        got = tok_all.at[2 * (1 - y) + m, c]
+        side.append(send(got, got, ss.at[k], rs.at[k], core))
+        k += 1
+    for m in range(2):
+        cps[m].wait_send()
+    for cp in cps[2:] + side:
+        cp.wait()
+
+
+def open_call(tok, seg, wqkv, gains):
+    return comm_call(
+        open_body,
+        "open_column",
+        1,
+        [((4, 2, 96, 1024), BF), ((2, 2, 1536), jnp.int32), ((2, 512, 768), BF), ((2, 8, 512), F32)],
+        [dma(14), dma(14)],
+        4,
+    )(tok, seg, wqkv, gains)
+
+
+def chips(b, c, y):
+    j = b // 2
+    res = []
+    for k in range(1, 8):
+        jd = (j + k) % 8
+        res.append((jd, (jd * 2 + c, y)))
+    return res
+
+
+def to_heads_body(qkv, up, att, up_sel, ss, rs):
+    b, y, z, x, c = place()
+    over = (b, 1 - y)
+    others = chips(b, c, y)
+    meet([over] + [peer for _, peer in others])
+    j = b // 2
+    cps = []
+    far = pl.multiple_of(((1 - y) * 2 + c) * 1024, 1024)
+    own = pl.multiple_of((y * 2 + c) * 1024, 1024)
+    cps.append(send(up.at[:, pl.ds(far, 1024)], up_sel.at[y], ss.at[0], rs.at[0], over))
+    for k, (jd, peer) in enumerate(others):
+        col = pl.multiple_of((jd % 2) * 384, 128)
+        cps.append(
+            send(qkv.at[jd // 2, :, pl.ds(col, 384)], att.at[j], ss.at[k + 1], rs.at[k + 1], peer)
+        )
+    att[j] = qkv[z, :, pl.ds(pl.multiple_of(x * 384, 128), 384)]
+    up_sel[y] = up[:, pl.ds(own, 1024)]
+    for cp in cps:
+        cp.wait()
+
+
+def to_heads(qkv, up):
+    return comm_call(
+        to_heads_body,
+        "to_heads",
+        2,
+        [((8, 192, 384), BF), ((2, 512, 1024), BF)],
+        [dma(8), dma(8)],
+        2,
+    )(qkv, up)
+
+
+def from_heads_body(attn, cot, rows, cot_all, ss, rs):
+    b, y, z, x, c = place()
+    core, over = (b + 1 - 2 * c, y), (b, 1 - y)
+    others = chips(b, c, y)
+    meet([core, over] + [peer for _, peer in others])
+    col = pl.multiple_of(x * 128, 128)
+    cps, side = [], []
+    for k, (jd, peer) in enumerate(others):
+        cps.append(send(attn.at[jd], rows.at[z, :, pl.ds(col, 128)], ss.at[k], rs.at[k], peer))
+    k = 7
+    near = []
+    for m in range(2):
+        near.append(send(cot.at[m], cot_all.at[2 * y + m, c], ss.at[k], rs.at[k], over))
+        k += 1
+    for m in range(2):
+        side.append(send(cot.at[m], cot_all.at[2 * y + m, c], ss.at[k], rs.at[k], core))
+        k += 1
+    rows[z, :, pl.ds(col, 128)] = attn[b // 2]
+    for m in range(2):
+        cot_all[2 * y + m, c] = cot[m]
+    for m in range(2):
+        near[m].wait_recv()
+        got = cot_all.at[2 * (1 - y) + m, c]
+        side.append(send(got, got, ss.at[k], rs.at[k], core))
+        k += 1
+    for cp in near:
+        cp.wait_send()
+    for cp in cps + side:
+        cp.wait()
+
+
+def from_heads(attn, cot):
+    return comm_call(
+        from_heads_body,
+        "from_heads",
+        3,
+        [((4, 192, 256), BF), ((4, 2, 96, 1024), BF)],
+        [dma(13), dma(13)],
+        2,
+    )(attn, cot)
+
+
+def column_sum(part, got, mid, fin, ss, rs, b, y, c):
+    core, over = (b + 1 - 2 * c, y), (b, 1 - y)
+    first = []
+    for m in range(2):
+        q = 2 * (1 - y) + m
+        first.append(send(part.at[q, 1 - c], got.at[q], ss.at[m], rs.at[m], core))
+    for m in range(2):
+        q = 2 * y + m
+        first.append(send(part.at[q, 1 - c], got.at[q], ss.at[2 + m], rs.at[2 + m], core))
+    second = []
+    for m in range(2):
+        q = 2 * (1 - y) + m
+        first[m].wait_recv()
+        mid[m] = (part[q, c].astype(F32) + got[q].astype(F32)).astype(BF)
+        second.append(send(mid.at[m], fin.at[m], ss.at[4 + m], rs.at[4 + m], over))
+    sums = []
+    for m in range(2):
+        q = 2 * y + m
+        first[2 + m].wait_recv()
+        second[m].wait_recv()
+        sums.append(part[q, c].astype(F32) + got[q].astype(F32) + fin[m].astype(F32))
+    for cp in first + second:
+        cp.wait_send()
+    return sums
+
+
+def column_spread(own, full, ss, rs, k, b, y, c):
+    core, over = (b + 1 - 2 * c, y), (b, 1 - y)
+    near, side = [], []
+    for m in range(2):
+        near.append(send(own.at[m], full.at[2 * y + m, c], ss.at[k], rs.at[k], over))
+        side.append(send(own.at[m], full.at[2 * y + m, c], ss.at[k + 1], rs.at[k + 1], core))
+        k += 2
+    for m in range(2):
+        full[2 * y + m, c] = own[m]
+    for m in range(2):
+        near[m].wait_recv()
+        got = full.at[2 * (1 - y) + m, c]
+        side.append(send(got, got, ss.at[k], rs.at[k], core))
+        k += 1
+    for cp in near:
+        cp.wait_send()
+    for cp in side:
+        cp.wait()
+
+
+SUM_SCRATCH = [
+    pltpu.VMEM((4, 96, 1024), BF),
+    pltpu.VMEM((2, 96, 1024), BF),
+    pltpu.VMEM((2, 96, 1024), BF),
+]
+
+
+def second_norm_body(part, tok, valid, gain, resid, h_all, got, mid, fin, own, ss, rs):
+    b, y, z, x, c = place()
+    meet([(b + 1 - 2 * c, y), (b, 1 - y)])
+    sums = column_sum(part, got, mid, fin, ss, rs, b, y, c)
+    for m in range(2):
+        res = tok[m].astype(F32) + valid[m][:, :1] * sums[m]
+        resid[m] = res
+        normed, _ = norm_rows(res)
+        own[m] = (normed * gain[1:2]).astype(BF)
+    column_spread(own, h_all, ss, rs, 6, b, y, c)
+
+
+def second_norm(part, tok, valid, gain):
+    return comm_call(
+        second_norm_body,
+        "second_norm",
+        4,
+        [((2, 96, 1024), F32), ((4, 2, 96, 1024), BF)],
+        SUM_SCRATCH + [pltpu.VMEM((2, 96, 1024), BF), dma(12), dma(12)],
+        4,
+    )(part, tok, valid, gain)
+
+
+def second_back_body(part, resid, cot, valid, gain, rgrad, ggrad, br_all, got, mid, fin, own, ss, rs):
+    b, y, z, x, c = place()
+    meet([(b + 1 - 2 * c, y), (b, 1 - y)])
+    sums = column_sum(part, got, mid, fin, ss, rs, b, y, c)
+    total = jnp.zeros((1, 1024), F32)
+    for m in range(2):
+        normed, inv_std = norm_rows(resid[m])
+        e = sums[m]
+        g = e * gain[1:2]
+        total = total + jnp.sum(e * normed, axis=0, keepdims=True)
+        one = jnp.mean(g, axis=-1, keepdims=True)
+        two = jnp.mean(g * normed, axis=-1, keepdims=True)
+        rg = cot[m].astype(F32) + (g - one - normed * two) * inv_std
+        rgrad[m] = rg
+        own[m] = (valid[m][:, :1] * rg).astype(BF)
+    ggrad[...] = jnp.broadcast_to(total, (8, 1024))
+    column_spread(own, br_all, ss, rs, 6, b, y, c)
+
+
+def second_back(part, resid, cot, valid, gain):
+    return comm_call(
+        second_back_body,
+        "second_back",
+        5,
+        [((2, 96, 1024), F32), ((8, 1024), F32), ((4, 2, 96, 1024), BF)],
+        SUM_SCRATCH + [pltpu.VMEM((2, 96, 1024), BF), dma(12), dma(12)],
+        5,
+    )(part, resid, cot, valid, gain)
+
+
+def grad_heads_body(agrad, part, resid, valid, do, out, got, mid, fin, ss, rs):
+    b, y, z, x, c = place()
+    others = chips(b, c, y)
+    meet([(b + 1 - 2 * c, y), (b, 1 - y)] + [peer for _, peer in others])
+    j = b // 2
+    cps = []
+    for k, (jd, peer) in enumerate(others):
+        col = pl.multiple_of((jd % 2) * 128, 128)
+        cps.append(
+            send(agrad.at[jd // 2, :, pl.ds(col, 128)], do.at[j], ss.at[6 + k], rs.at[6 + k], peer)
+        )
+    do[j] = agrad[z, :, pl.ds(pl.multiple_of(x * 128, 128), 128)]
+    sums = column_sum(part, got, mid, fin, ss, rs, b, y, c)
+    for m in range(2):
+        out[m] = (resid[m] + valid[m][:, :1] * sums[m]).astype(BF)
+    for cp in cps:
+        cp.wait()
+
+
+def grad_heads(agrad, part, resid, valid):
+    return comm_call(
+        grad_heads_body,
+        "grad_heads",
+        6,
+        [((8, 192, 128), BF), ((2, 96, 1024), BF)],
+        SUM_SCRATCH + [dma(13), dma(13)],
+        4,
+    )(agrad, part, resid, valid)
+
+
+def grad_rows_body(dqkv, rows, ss, rs):
+    b, y, z, x, c = place()
+    others = chips(b, c, y)
+    meet([peer for _, peer in others])
+    col = pl.multiple_of(x * 384, 128)
+    cps = []
+    for k, (jd, peer) in enumerate(others):
+        cps.append(send(dqkv.at[jd], rows.at[z, :, pl.ds(col, 384)], ss.at[k], rs.at[k], peer))
+    rows[z, :, pl.ds(col, 384)] = dqkv[b // 2]
+    for cp in cps:
+        cp.wait()
+
+
+def grad_rows(dqkv):
+    return comm_call(
+        grad_rows_body, "grad_rows", 7, [((4, 192, 768), BF)], [dma(7), dma(7)], 1
+    )(dqkv)[0]
+
+
+def first_back_body(part, tok, rgrad, gain, tgrad, ggrad, got, mid, fin, ss, rs):
+    b, y, z, x, c = place()
+    meet([(b + 1 - 2 * c, y), (b, 1 - y)])
+    sums = column_sum(part, got, mid, fin, ss, rs, b, y, c)
+    total = jnp.zeros((1, 1024), F32)
+    for m in range(2):
+        normed, inv_std = norm_rows(tok[m].astype(F32))
+        e = sums[m]
+        g = e * gain[0:1]
+        total = total + jnp.sum(e * normed, axis=0, keepdims=True)
+        one = jnp.mean(g, axis=-1, keepdims=True)
+        two = jnp.mean(g * normed, axis=-1, keepdims=True)
+        tgrad[m] = rgrad[m] + (g - one - normed * two) * inv_std
+    ggrad[...] = jnp.broadcast_to(total, (8, 1024))
+
+
+def first_back(part, tok, rgrad, gain):
+    return comm_call(
+        first_back_body,
+        "first_back",
+        8,
+        [((2, 96, 1024), F32), ((8, 1024), F32)],
+        SUM_SCRATCH + [dma(6), dma(6)],
+        4,
+    )(part, tok, rgrad, gain)
+
+
+def last_dot(a, b):
+    return lax.dot_general(a, b, (((1,), (1,)), ((), ())), preferred_element_type=F32)
+
+
+def plain_dot(a, b):
+    return lax.dot_general(a, b, (((1,), (0,)), ((), ())), preferred_element_type=F32)
+
+
+def attend_body(qkv, seg_col, seg_row, out_low, out, lse):
+    rows = out.shape[0]
+    i = pl.program_id(0)
+    at = pl.multiple_of(i * rows, rows)
+    q = qkv[pl.ds(at, rows), 0:128]
+    keys = qkv[:, 128:256]
+    values = qkv[:, 256:384]
+    low_half = lax.broadcasted_iota(jnp.int32, (rows, 128), 1) < HEAD_DIM
+    mask = seg_col[:, 0:1] == seg_row[0:1, :]
+    outs, norms = [], []
+    for h in range(2):
+        qh = jnp.where(low_half if h == 0 else ~low_half, q * SCALE, 0.0).astype(BF)
+        scores = jnp.where(mask, last_dot(qh, keys), NEG)
+        top = jnp.max(scores, axis=-1, keepdims=True)
+        probs = jnp.exp(scores - top)
+        total = jnp.sum(probs, axis=-1, keepdims=True)
+        outs.append(plain_dot(probs.astype(BF), values) / total)
+        norms.append(top + jnp.log(total))
+    res = jnp.where(low_half, outs[0], outs[1])
+    out[...] = res
+    out_low[...] = res.astype(BF)
+    lse[...] = jnp.where(low_half, norms[0], norms[1])
+
+
+def attend(qkv, seg_col, seg_row):
+    length = qkv.shape[0]
+    rows = 256
+    tile = pl.BlockSpec((rows, 128), lambda i: (i, 0))
+    return pl.pallas_call(
+        attend_body,
+        grid=(length // rows,),
+        in_specs=[
+            pl.BlockSpec((length, 384), lambda i: (0, 0)),
+            pl.BlockSpec((rows, 128), lambda i: (i, 0)),
+            pl.BlockSpec((8, length), lambda i: (0, 0)),
+        ],
+        out_specs=[tile, tile, tile],
+        out_shape=[
+            jax.ShapeDtypeStruct((length, 128), BF),
+            jax.ShapeDtypeStruct((length, 128), F32),
+            jax.ShapeDtypeStruct((length, 128), F32),
+        ],
+        name="attend",
+    )(qkv, seg_col, seg_row)
+
+
+def attend_back_body(qkv, out, lse, do, seg_col, seg_row, dqkv, lse_t, delta, keys_t, dq_t):
+    length = qkv.shape[0]
+    rows = seg_col.shape[0]
+    i = pl.program_id(0)
+    at = pl.multiple_of(i * rows, rows)
+
+    @pl.when(i == 0)
+    def _():
+        lse_t[...] = jnp.transpose(lse[...])
+        prod = jnp.transpose(do[...].astype(F32) * out[...])
+        delta[0:8] = jnp.broadcast_to(jnp.sum(prod[:HEAD_DIM], axis=0, keepdims=True), (8, length))
+        delta[8:16] = jnp.broadcast_to(jnp.sum(prod[HEAD_DIM:], axis=0, keepdims=True), (8, length))
+        keys_t[...] = jnp.transpose(qkv[:, 128:256].astype(F32)).astype(BF)
+        dq_t[...] = jnp.zeros_like(dq_t)
+
+    keys = qkv[pl.ds(at, rows), 128:256]
+    values = qkv[pl.ds(at, rows), 256:384]
+    q = qkv[:, 0:128]
+    douts = do[...]
+    low_half = lax.broadcasted_iota(jnp.int32, (rows, 128), 1) < HEAD_DIM
+    low_rows = lax.broadcasted_iota(jnp.int32, (128, 1), 0) < HEAD_DIM
+    mask = seg_col[:, 0:1] == seg_row[0:1, :]
+    kgrads, vgrads, qgrads = [], [], []
+    for h in range(2):
+        pick = low_half if h == 0 else ~low_half
+        kh = jnp.where(pick, keys * SCALE, 0.0).astype(BF)
+        vh = jnp.where(pick, values, 0.0).astype(BF)
+        scores = last_dot(kh, q)
+        probs = jnp.where(mask, jnp.exp(scores - lse_t[h * HEAD_DIM : h * HEAD_DIM + 1]), 0.0)
+        vgrads.append(plain_dot(probs.astype(BF), douts))
+        pgrad = last_dot(vh, douts)
+        sgrad = (probs * (pgrad - delta[h * 8 : h * 8 + 1])).astype(BF)
+        kgrads.append(plain_dot(sgrad, q))
+        qgrads.append(plain_dot(keys_t[:, pl.ds(at, rows)], sgrad))
+    dq_t[...] += jnp.where(low_rows, qgrads[0], qgrads[1])
+    dqkv[pl.ds(at, rows), 128:256] = (jnp.where(low_half, kgrads[0], kgrads[1]) * SCALE).astype(BF)
+    dqkv[pl.ds(at, rows), 256:384] = jnp.where(low_half, vgrads[0], vgrads[1]).astype(BF)
+
+    @pl.when(i == pl.num_programs(0) - 1)
+    def _():
+        dqkv[:, 0:128] = (jnp.transpose(dq_t[...]) * SCALE).astype(BF)
+
+
+def attend_back(qkv, out, lse, do, seg_col, seg_row):
+    length = qkv.shape[0]
+    rows = 256
+    whole = pl.BlockSpec((length, 128), lambda i: (0, 0))
+    wide = pl.BlockSpec((length, 384), lambda i: (0, 0))
+    return pl.pallas_call(
+        attend_back_body,
+        grid=(length // rows,),
+        in_specs=[
+            wide,
+            whole,
+            whole,
+            whole,
+            pl.BlockSpec((rows, 128), lambda i: (i, 0)),
+            pl.BlockSpec((8, length), lambda i: (0, 0)),
+        ],
+        out_specs=wide,
+        out_shape=jax.ShapeDtypeStruct((length, 384), BF),
+        scratch_shapes=[
+            pltpu.VMEM((128, length), F32),
+            pltpu.VMEM((16, length), F32),
+            pltpu.VMEM((128, length), BF),
+            pltpu.VMEM((128, length), F32),
+        ],
+        name="attend_back",
+    )(qkv, out, lse, do, seg_col, seg_row)
+
+
+def flip(v, bit):
+    return lax.ppermute(v, "band", [(i, i ^ bit) for i in range(16)])
+
+
+def keep_half(v, bit_value, bit):
+    half = v.shape[1] // 2
+    mine = lax.dynamic_slice_in_dim(v, bit_value * half, half, 1)
+    theirs = lax.dynamic_slice_in_dim(v, (1 - bit_value) * half, half, 1)
+    return mine.astype(F32) + flip(theirs.astype(BF), bit).astype(F32)
+
+
+def join_half(v, bit_value, bit):
+    other = flip(v, bit)
+    return jnp.where(
+        bit_value == 0,
+        jnp.concatenate([v, other], axis=1),
+        jnp.concatenate([other, v], axis=1),
+    )
+
+
+def reduce_columns(v, halves):
+    b, y, z, x, c = place()
+    bits = ((x, 2), (z % 2, 4), (z // 2, 8))
+    for value, bit in bits:
+        v = keep_half(v, value, bit)
+    v = v.astype(BF)
+    if halves:
+        mine = lax.dynamic_slice_in_dim(v, y, 1, 0)
+        theirs = lax.ppermute(lax.dynamic_slice_in_dim(v, 1 - y, 1, 0), "seq", [(0, 1), (1, 0)])
+        v = jnp.where(
+            y == 0, jnp.concatenate([mine, theirs], 0), jnp.concatenate([theirs, mine], 0)
+        )
+    for value, bit in reversed(bits):
+        v = join_half(v, value, bit)
+    v = v[None]
+    other = flip(v, 1)
+    return jnp.where(c == 0, jnp.concatenate([v, other], 0), jnp.concatenate([other, v], 0))
+
+
+def column_device(
+    tokens,
+    segment_ids,
+    qkv_weight,
+    out_weight,
+    up_weight,
+    down_weight,
+    gain_first,
+    gain_second,
+    out_cotangent,
+):
+    b, y, z, x, c = place()
+    my_seg = lax.dynamic_slice_in_dim(segment_ids, b * 96, 96, 1)
+    valid = jnp.broadcast_to((my_seg >= 0).astype(F32)[:, :, None], (2, 96, 128))
+    gains = jnp.pad(jnp.stack([gain_first, gain_second]).astype(F32), ((0, 6), (0, 0)))
+    tok_all, seg_all, w_sel, gains_all = open_call(tokens, segment_ids, qkv_weight, gains)
+    gain = jnp.transpose(gains_all, (1, 0, 2)).reshape(8, 1024)
+    seg_all = seg_all.reshape(4, 1536)
+    seg_z = lax.dynamic_slice_in_dim(seg_all, z, 1, 0)
+    seg_row = jnp.broadcast_to(seg_z, (8, 1536))
+    seg_col = jnp.broadcast_to(seg_z.reshape(1536, 1), (1536, 128))
+    seg_here = lax.dynamic_slice_in_dim(seg_all, (z * 2 + x) * 192, 192, 1)
+    valid_all = (seg_here >= 0).astype(F32).reshape(768, 1)
+    w_sel = w_sel.reshape(1024, 768)
+    normed, _ = norm_rows(tok_all.reshape(768, 1024).astype(F32))
+    h_one = (normed * gain[0:1]).astype(BF)
+    qkv = plain_dot(h_one, w_sel).astype(BF)
+    att, up_sel = to_heads(qkv.reshape(4, 192, 768), up_weight)
+    up_sel = up_sel.reshape(1024, 1024)
+    att = att.reshape(1536, 384)
+    out_low, out_full, lse = attend(att, seg_col, seg_row)
+    attn_low, cot_all = from_heads(out_low.reshape(8, 192, 128), out_cotangent)
+    attn_low = attn_low.reshape(768, 256)
+    out_rows = lax.dynamic_slice_in_dim(out_weight, c * 256, 256, 0)
+    part = plain_dot(attn_low, out_rows).astype(BF)
+    resid, h_two = second_norm(part.reshape(4, 2, 96, 1024), tokens, valid, gain)
+    h_two = h_two.reshape(768, 1024)
+    pre_act = plain_dot(h_two, up_sel)
+    hidden_low = jax.nn.gelu(pre_act, approximate=False).astype(BF)
+    down_rows = lax.dynamic_slice_in_dim(down_weight, c * 1024, 1024, 0)
+    grad_two = (valid_all * cot_all.reshape(768, 1024).astype(F32)).astype(BF)
+    hidden_grad = last_dot(grad_two, down_rows)
+    slope = 0.5 * (1.0 + lax.erf(pre_act * ROOT_HALF)) + pre_act * DENSITY * jnp.exp(
+        -0.5 * pre_act * pre_act
+    )
+    pre_grad = (hidden_grad * slope).astype(BF)
+    e_part = last_dot(pre_grad, up_sel).astype(BF)
+    rgrad, gain_two_grad, branch = second_back(
+        e_part.reshape(4, 2, 96, 1024), resid, out_cotangent, valid, gain
+    )
+    branch = branch.reshape(768, 1024)
+    branch_two = plain_dot(hidden_low, down_rows).astype(BF)
+    first_dot = lambda a, d: lax.dot_general(
+        a, d, (((0,), (0,)), ((), ())), preferred_element_type=F32
+    )
+    down_grad = first_dot(hidden_low, grad_two)
+    up_grad = first_dot(h_two, pre_grad)
+    down_sum = reduce_columns(down_grad.reshape(1, 1024, 1024), False)
+    up_sum = reduce_columns(up_grad.reshape(2, 512, 1024), True)
+    attn_grad = last_dot(branch, out_rows).astype(BF)
+    do, layer_out = grad_heads(
+        attn_grad.reshape(4, 192, 256), branch_two.reshape(4, 2, 96, 1024), resid, valid
+    )
+    outproj_grad = first_dot(attn_low, branch)
+    out_sum = reduce_columns(outproj_grad.reshape(1, 256, 1024), False)
+    dqkv = attend_back(att, out_full, lse, do.reshape(1536, 128), seg_col, seg_row)
+    dqkv_rows = grad_rows(dqkv.reshape(8, 192, 384)).reshape(768, 768)
+    c_part = last_dot(dqkv_rows, w_sel).astype(BF)
+    token_grad, gain_one_grad = first_back(c_part.reshape(4, 2, 96, 1024), tokens, rgrad, gain)
+    qkv_grad = first_dot(h_one, dqkv_rows)
+    qkv_sum = reduce_columns(qkv_grad.reshape(2, 512, 768), True)
+    both = lax.psum(jnp.stack([gain_one_grad[0], gain_two_grad[0]]), ("band", "seq"))
+    gain_out = lax.dynamic_slice_in_dim(both, y * 512, 512, 1)
+    qkv_out = jnp.transpose(qkv_sum.reshape(2, 2, 512, 2, 3, 128), (2, 4, 1, 0, 3, 5))
+    up_out = jnp.transpose(up_sum, (2, 1, 0, 3))
+    return (
+        layer_out,
+        token_grad,
+        qkv_out.reshape(512, 3072).astype(F32),
+        out_sum.reshape(512, 1024).astype(F32),
+        up_out.reshape(512, 4096).astype(F32),
+        down_sum.reshape(2048, 1024).astype(F32),
+        gain_out[0],
+        gain_out[1],
+    )
+
+
 def solution(mesh):
     placed = (
         P("seq", "band", None),
@@ -340,8 +961,9 @@
         P("seq"),
         P("seq", "band", None),
     )
+    split = dict(mesh.shape) == {"band": 16, "seq": 2}
     return jax.shard_map(
-        per_device,
+        column_device if split else per_device,
         mesh=mesh,
         in_specs=placed,
         out_specs=(

time: 1320 us -> 624 us (0.47)
  waiting for transfers between devices: 902 us -> 83.4 us
  Pallas kernels: 0 us -> 242 us
  matrix products: 157 us -> 50.9 us
  local copies, waits for them, and re-layouts: 131 us -> 67.6 us
  starting transfers between devices: 0.48 us -> 41.5 us
  blocking collectives: 48.8 us -> 65.6 us
  between operations: 15.5 us -> 1.68 us
    all_gather x6 -> x0, waiting for transfers between devices: 358 us -> none  [the longest x1 96.3 us: per_device(): lax.all_gather(down_weight, 'seq', axis=0, tiled=True)]
    reduce_scatter x5 -> x0, waiting for transfers between devices: 356 us -> none  [the longest x1 102 us: per_device(): lax.psum_scatter(up_grad.astype(jnp.bfloat16), 'seq', scatter_dimension=0...]
    pallas_call x0 -> x10, Pallas kernels: none -> 242 us  [the longest x1 34.2 us: open_call(): comm_call(open_body, 'open_column', 1, [((4, 2, 96, 1024), BF), ((2, 2, 1...]
    psum x1 -> x0, waiting for transfers between devices: 184 us -> none  [per_device(): lax.psum(shares[0].astype(jnp.bfloat16), 'band').astype(jnp.float32)]
    dot_general x68 -> x12, matrix products: 157 us -> 50.9 us  [the longest x4 20.1 us: plain_dot(): lax.dot_general(a, b, (((1,), (0,)), ((), ())), preferred_element_type=F32)]
    ppermute x0 -> x30, waiting for transfers between devices: none -> 83.4 us  [the longest x28 83.4 us: flip(): return lax.ppermute(v, 'band', [(i, i ^ bit) for i in range(16)])]
    dynamic_slice x48 -> x3, local copies, waits for them, and re-layouts: 50.3 us -> 0.08 us  [the longest x2 0.05 us: reduce_columns(): mine = lax.dynamic_slice_in_dim(v, y, 1, 0)]
    ppermute x0 -> x30, starting transfers between devices: none -> 41.5 us  [the longest x28 40.1 us: flip(): return lax.ppermute(v, 'band', [(i, i ^ bit) for i in range(16)])]
  transfers between devices with their start and end apart: 12 -> 30, of which waited for: 11 -> 10; matrix products, arithmetic and copies ran while one was open for 14% -> 19% of each run, Pallas kernels for 0% -> 14%
where the time goes in v1:
time: 624 us; the launch traced here: 619 us
  Pallas kernels  242 us (39%)
  waiting for transfers between devices  83.4 us (13%)
  local copies, waits for them, and re-layouts  67.6 us (11%)
  other arithmetic  66.9 us (11%)
  blocking collectives  65.6 us (11%)
  matrix products  50.9 us (8%)
  starting transfers between devices  41.5 us (7%)
    ppermute x28, waiting for transfers between devices, flip(): return lax.ppermute(v, 'band', [(i, i ^ bit) for i in range(16)])  83.4 us
    psum x1, blocking collectives, column_device(): lax.psum(jnp.stack([gain_one_grad[0], gain_two_grad[0]]), ('band', 'seq'))  65.6 us
    ppermute x28, starting transfers between devices, flip(): return lax.ppermute(v, 'band', [(i, i ^ bit) for i in range(16)])  40.1 us
    pallas_call x1, Pallas kernels, open_call(): comm_call(open_body, 'open_column', 1, [((4, 2, 96, 1024), BF), ((2, 2, 1...  34.2 us
    pallas_call x1, Pallas kernels, to_heads(): comm_call(to_heads_body, 'to_heads', 2, [((8, 192, 384), BF), ((2, 512, 1...  32 us
    pallas_call x1, Pallas kernels, grad_heads(): comm_call(grad_heads_body, 'grad_heads', 6, [((8, 192, 128), BF), ((2, 96...  31.6 us
    pallas_call x1, Pallas kernels, second_norm(): comm_call(second_norm_body, 'second_norm', 4, [((2, 96, 1024), F32), ((4,...  28.5 us
    pallas_call x1, Pallas kernels, second_back(): comm_call(second_back_body, 'second_back', 5, [((2, 96, 1024), F32), ((8,...  27.4 us
  transfers between devices with their start and end apart: 30, of which 10 were waited for; matrix products, arithmetic and copies ran while one was open for 19% of the time, Pallas kernels for 14%

profile of v1, /device:TPU:0, one launch (start us, length us, event | category | flops | bytes accessed | tf_op | source)
XLA Modules:
  0.0 619.4 jit_solution(8391439062437967101)
XLA Ops:
  3.5 34.2 %open_column.1 = (bf16[4,2,96,1024]{3,2,1,0:T(8,128)(2,1)}, s32[2,2,1536]{2,1,0:T(2,128)}, bf16[2,512,768]{2,1,0:T(8,128)(2,1)}, f32[2,8,512]{2,1,0:T(8,128)}) custom-call(bf16[2,96,1024]{2,1,0:T(8,128)(2,1)} %tok.5, s32[2,1536]{1,0:T(2,128)} %seg.1, bf16[512,3072]{1,0:T(8,128)(2,1)} %wqkv.1, f32[8,512]{1,0:T(8,128)} %fusion.41.gains), custom_call_target="tpu_custom_call" | custom-call | tf_op jit(solution)/shard_map/open_column/pallas_call | solution.py:426
  47.1 32.0 %to_heads.1 = (bf16[8,192,384]{2,1,0:T(8,128)(2,1)}, bf16[2,512,1024]{2,1,0:T(8,128)(2,1)}) custom-call(bf16[4,192,768]{2,1,0:T(8,128)(2,1)} %bitcast.137, bf16[512,4096]{1,0:T(8,128)(2,1)} %up.1), custom_call_target="tpu_custom_call" | custom-call | tf_op jit(solution)/shard_map/to_heads/pallas_call | solution.py:467
  80.9 12.6 %attend.1 = (bf16[1536,128]{1,0:T(8,128)(2,1)}, f32[1536,128]{1,0:T(8,128)}, f32[1536,128]{1,0:T(8,128)}) custom-call(bf16[1536,384]{1,0:T(8,128)(2,1)} %bitcast.111, s32[1536,128]{1,0:T(8,128)} %broadcast_in_dim.9.seg_col, s32[8,1536]{1,0:T(8,128)} %broadcast_in_dim.10.seg_row), custom_call_target="tpu_custom_call" | custom-call | tf_op jit(solution)/shard_map/attend/pallas_call | solution.py:737
  93.5 17.6 %from_heads.1 = (bf16[4,192,256]{2,1,0:T(8,128)(2,1)}, bf16[4,2,96,1024]{3,2,1,0:T(8,128)(2,1)}) custom-call(bf16[8,192,128]{2,1,0:T(8,128)(2,1)} %bitcast.142, bf16[2,96,1024]{2,1,0:T(8,128)(2,1)} %cot.3), custom_call_target="tpu_custom_call" | custom-call | tf_op jit(solution)/shard_map/from_heads/pallas_call | solution.py:509
  116.6 28.5 %second_norm.1 = (f32[2,96,1024]{2,1,0:T(8,128)}, bf16[4,2,96,1024]{3,2,1,0:T(8,128)(2,1)}) custom-call(bf16[4,2,96,1024]{3,2,1,0:T(8,128)(2,1)} %bitcast.110, bf16[2,96,1024]{2,1,0:T(8,128)(2,1)} %tok.5, f32[2,96,128]{2,1,0:T(8,128)} %broadcast_in_dim.11.valid, f32[8,1024]{1,0:T(8,128)} %bitcast.145), custom_call_target="tpu_custom_call" | custom-call | tf_op jit(solution)/shard_map/second_norm/pallas_call | solution.py:585
  145.1 11.0 %fusion.7 = (bf16[768,1024]{1,0:T(8,128)(2,1)}, f32[768,1024]{1,0:T(8,128)S(1)}) fusion(bf16[768,1024]{1,0:T(8,128)(2,1)} %bitcast.124, bf16[1024,1024]{1,0:T(8,128)(2,1)} %bitcast.153), kind=kOutput, calls=%fused_computation.15 | convolution fusion | flops 1661730816 | bytes 8388608 | tf_op jit(solution)/shard_map/dot_general | solution.py:706
  162.4 27.4 %second_back.1 = (f32[2,96,1024]{2,1,0:T(8,128)}, f32[8,1024]{1,0:T(8,128)}, bf16[4,2,96,1024]{3,2,1,0:T(8,128)(2,1)}) custom-call(bf16[4,2,96,1024]{3,2,1,0:T(8,128)(2,1)} %bitcast.131, f32[2,96,1024]{2,1,0:T(8,128)} %get-tuple-element.38.resid, bf16[2,96,1024]{2,1,0:T(8,128)(2,1)} %cot.3, f32[2,96,128]{2,1,0:T(8,128)} %broadcast_in_dim.11.valid, ...), custom_call_target="tpu_custom_call" | custom-call | tf_op jit(solution)/shard_map/second_back/pallas_call | solution.py:615
  197.8 5.7 fusion.25
  207.6 5.7 fusion.48
  216.9 5.0 fusion.22
  227.7 31.6 %grad_heads.1 = (bf16[8,192,128]{2,1,0:T(8,128)(2,1)}, bf16[2,96,1024]{2,1,0:T(8,128)(2,1)}) custom-call(bf16[4,192,256]{2,1,0:T(8,128)(2,1)} %bitcast.143, bf16[4,2,96,1024]{3,2,1,0:T(8,128)(2,1)} %bitcast.130, f32[2,96,1024]{2,1,0:T(8,128)} %get-tuple-element.38.resid, f32[2,96,128]{2,1,0:T(8,128)} %broadcast_in_dim.11.valid), custom_call_target="tpu_custom_call" | custom-call | tf_op jit(solution)/shard_map/grad_heads/pallas_call | solution.py:645
  259.3 17.4 %attend_back.1 = bf16[1536,384]{1,0:T(8,128)(2,1)} custom-call(bf16[1536,384]{1,0:T(8,128)(2,1)} %bitcast.112, f32[1536,128]{1,0:T(8,128)} %get-tuple-element.41.out, f32[1536,128]{1,0:T(8,128)} %get-tuple-element.42.lse, bf16[1536,128]{1,0:T(8,128)(2,1)} %bitcast.141, s32[1536,128]{1,0:T(8,128)} %broadcast_in_dim.9.seg_col, s32[8,1536]{1,0:T(8,128)} %broadcast_in_dim.10.seg_row), custom_call_target="tpu_custom_call" | custom-call | tf_op jit(solution)/shard_map/attend_back/pallas_call | solution.py:803
  276.7 24.2 %grad_rows.1 = bf16[4,192,768]{2,1,0:T(8,128)(2,1)} custom-call(bf16[8,192,384]{2,1,0:T(8,128)(2,1)} %bitcast.113), custom_call_target="tpu_custom_call" | custom-call | tf_op jit(solution)/shard_map/grad_rows/pallas_call | solution.py:669
  301.1 6.9 %collective-permute-start.9 = (bf16[1,64,1024]{2,1,0:T(8,128)(2,1)S(1)}, bf16[1,64,1024]{2,1,0:T(8,128)(2,1)S(1)}, u32[]{:S(2)}, u32[]{:S(2)}) collective-permute-start(bf16[1,64,1024]{2,1,0:T(8,128)(2,1)S(1)} %dynamic-slice_convert_fusion.10), channel_id=1, source_target_pairs={{0,8},{2,10},{4,12},{6,14},{8,0},{10,2},{12,4},{14,6},{16,24},{18,... | collective-permute-start | bytes 393224 | tf_op jit(solution)/shard_map/ppermute | solution.py:827
  324.9 16.2 %first_back.1 = (f32[2,96,1024]{2,1,0:T(8,128)}, f32[8,1024]{1,0:T(8,128)}) custom-call(bf16[4,2,96,1024]{3,2,1,0:T(8,128)(2,1)} %bitcast.129, bf16[2,96,1024]{2,1,0:T(8,128)(2,1)} %tok.5, f32[2,96,1024]{2,1,0:T(8,128)} %get-tuple-element.44.rgrad, f32[8,1024]{1,0:T(8,128)} %bitcast.147), custom_call_target="tpu_custom_call" | custom-call | tf_op jit(solution)/shard_map/first_back/pallas_call | solution.py:691
  348.8 8.0 %collective-permute-done.1 = bf16[2,128,768]{2,1,0:T(8,128)(2,1)S(1)} collective-permute-done((bf16[2,128,768]{2,1,0:T(8,128)(2,1)S(1)}, bf16[2,128,768]{2,1,0:T(8,128)(2,1)S(1)}, u32[]{:S(2)}, u32[]{:S(2)}) %collective-permute-start.1) | collective-permute-done | bytes 393248 | tf_op jit(solution)/shard_map/ppermute | solution.py:827
  361.9 8.9 %collective-permute-done.2 = bf16[2,64,768]{2,1,0:T(8,128)(2,1)S(1)} collective-permute-done((bf16[2,64,768]{2,1,0:T(8,128)(2,1)S(1)}, bf16[2,64,768]{2,1,0:T(8,128)(2,1)S(1)}, u32[]{:S(2)}, u32[]{:S(2)}) %collective-permute-start.2) | collective-permute-done | bytes 196640 | tf_op jit(solution)/shard_map/ppermute | solution.py:827
  374.5 13.5 %collective-permute-done.16 = bf16[2,128,1024]{2,1,0:T(8,128)(2,1)S(1)} collective-permute-done((bf16[2,128,1024]{2,1,0:T(8,128)(2,1)S(1)}, bf16[2,128,1024]{2,1,0:T(8,128)(2,1)S(1)}, u32[]{:S(2)}, u32[]{:S(2)}) %collective-permute-start.16) | collective-permute-done | bytes 524320 | tf_op jit(solution)/shard_map/ppermute | solution.py:827
  391.8 19.6 %collective-permute-done.17 = bf16[2,64,1024]{2,1,0:T(8,128)(2,1)S(1)} collective-permute-done((bf16[2,64,1024]{2,1,0:T(8,128)(2,1)S(1)}, bf16[2,64,1024]{2,1,0:T(8,128)(2,1)S(1)}, u32[]{:S(2)}, u32[]{:S(2)}) %collective-permute-start.17) | collective-permute-done | bytes 262176 | tf_op jit(solution)/shard_map/ppermute | solution.py:827
  411.4 5.5 collective-permute-done.26
  427.2 10.8 %collective-permute-done.27 = bf16[1,256,1024]{2,1,0:T(8,128)(2,1)S(1)} collective-permute-done((bf16[1,256,1024]{2,1,0:T(8,128)(2,1)S(1)}, bf16[1,256,1024]{2,1,0:T(8,128)(2,1)S(1)}, u32[]{:S(2)}, u32[]{:S(2)}) %collective-permute-start.27) | collective-permute-done | bytes 524320 | tf_op jit(solution)/shard_map/ppermute | solution.py:827
  442.0 4.4 collective-permute-done.5
  449.5 65.6 %psum.7 = f32[2,1024]{1,0:T(2,128)S(1)} all-reduce(f32[2,1024]{1,0:T(2,128)S(1)} %pad_maximum_fusion), channel_id=1, replica_groups=mesh['band'=16,'seq'=2] {'band','seq'}, use_global_device_ids=true, to_apply=%region_2.3 | all-reduce | flops 2048 | bytes 16384 | tf_op jit(solution)/shard_map/psum | solution.py:936
  538.0 8.6 %collective-permute-done.21 = bf16[2,256,1024]{2,1,0:T(8,128)(2,1)} collective-permute-done((bf16[2,256,1024]{2,1,0:T(8,128)(2,1)S(1)}, bf16[2,256,1024]{2,1,0:T(8,128)(2,1)}, u32[]{:S(2)}, u32[]{:S(2)}) %collective-permute-start.21) | collective-permute-done | bytes 1048608 | tf_op jit(solution)/shard_map/ppermute | solution.py:827
  559.4 7.8 %convert_bitcast_fusion.1 = f32[512,3,2,2,2,128]{5,1,4,0,2,3:T(4,128)} fusion(bf16[1,2,512,2,3,128]{5,4,3,2,1,0:T(4,128)(2,1)S(1)} %copy.41, bf16[1,2,512,2,3,128]{5,4,3,2,1,0:T(4,128)(2,1)} %maximum_select_fusion.3, pred[]{:T(512)S(6)} %eq.43), kind=kLoop, calls=%fused_computation.1 | loop fusion | flops 6291456 | bytes 9437185 | tf_op jit(solution)/shard_map/convert_element_type | solution.py:943
  567.2 9.0 %copy.43 = f32[512,3,2,2,2,128]{0,5,4,3,2,1:T(8,128)} copy(f32[512,3,2,2,2,128]{5,1,4,0,2,3:T(4,128)} %convert_bitcast_fusion.1) | data formatting | bytes 12582912 | tf_op jit(solution)/shard_map/convert_element_type | solution.py:943
  576.2 6.6 %copy.46 = f32[512,3072]{1,0:T(8,128)} copy(f32[512,3072]{0,1:T(8,128)} %bitcast.107) | data formatting | bytes 12582912
  582.7 4.7 maximum_select_fusion.2
  587.4 4.7 bitcast_convert_fusion
  592.2 7.5 %convert_bitcast_fusion = f32[512,2,2,1024]{3,0,1,2:T(8,128)} fusion(bf16[1,2,512,1024]{3,2,1,0:T(8,128)(2,1)} %collective-permute-done.22, bf16[1,2,512,1024]{3,2,1,0:T(8,128)(2,1)} %maximum_select_fusion.4, pred[]{:T(512)S(6)} %eq.43), kind=kLoop, calls=%fused_computation | loop fusion | flops 8388608 | bytes 12582913 | tf_op jit(solution)/shard_map/convert_element_type | solution.py:945
  599.7 8.8 %copy.45 = f32[512,2,2,1024]{0,3,2,1:T(8,128)} copy(f32[512,2,2,1024]{3,0,1,2:T(8,128)} %convert_bitcast_fusion) | data formatting | bytes 16777216 | tf_op jit(solution)/shard_map/convert_element_type | solution.py:945
  608.4 9.1 %copy.47 = f32[512,4096]{1,0:T(8,128)} copy(f32[512,4096]{0,1:T(8,128)} %bitcast.106) | data formatting | bytes 16777216
  (187 shorter events, 138.5 us)
Async XLA Ops:
  0.6 113.5 %copy-start = (bf16[512,1024]{1,0:T(8,128)(2,1)S(1)}, bf16[512,1024]{1,0:T(8,128)(2,1)}, u32[]{:S(2)}) copy-start(bf16[512,1024]{1,0:T(8,128)(2,1)} %param.12) | copy-start | bytes 3145732
  194.6 106.4 %collective-permute-start.8 = (bf16[1,128,1024]{2,1,0:T(8,128)(2,1)}, bf16[1,128,1024]{2,1,0:T(8,128)(2,1)S(1)}, u32[]{:S(2)}, u32[]{:S(2)}) collective-permute-start(bf16[1,128,1024]{2,1,0:T(8,128)(2,1)} %fusion.32), channel_id=1, source_target_pairs={{0,4},{2,6},{4,0},{6,2},{8,12},{10,14},{12,8},{14,10},{16,20},{18,... | collective-permute-start | bytes 786440 | tf_op jit(solution)/shard_map/ppermute | solution.py:827
  206.2 152.9 %collective-permute-start.15 = (bf16[2,256,1024]{2,1,0:T(8,128)(2,1)}, bf16[2,256,1024]{2,1,0:T(8,128)(2,1)}, u32[]{:S(2)}, u32[]{:S(2)}) collective-permute-start(bf16[2,256,1024]{2,1,0:T(8,128)(2,1)} %dynamic-slice_convert_fusion.1), channel_id=1, source_target_pairs={{0,4},{2,6},{4,0},{6,2},{8,12},{10,14},{12,8},{14,10},{16,20},{18,... | collective-permute-start | bytes 3145736 | tf_op jit(solution)/shard_map/ppermute | solution.py:827
  216.2 129.6 %collective-permute-start.23 = (bf16[1,512,1024]{2,1,0:T(8,128)(2,1)}, bf16[1,512,1024]{2,1,0:T(8,128)(2,1)}, u32[]{:S(2)}, u32[]{:S(2)}) collective-permute-start(bf16[1,512,1024]{2,1,0:T(8,128)(2,1)} %fusion.27), channel_id=1, source_target_pairs={{0,4},{2,6},{4,0},{6,2},{8,12},{10,14},{12,8},{14,10},{16,20},{18,... | collective-permute-start | bytes 3145736 | tf_op jit(solution)/shard_map/ppermute | solution.py:827
  259.3 41.6 %copy-start.3 = (f32[256,1024]{1,0:T(8,128)S(1)}, f32[256,1024]{1,0:T(8,128)}, u32[]{:S(2)}) copy-start(f32[256,1024]{1,0:T(8,128)} %fusion.47) | copy-start | bytes 3145732
  301.1 11.2 %collective-permute-start.9 = (bf16[1,64,1024]{2,1,0:T(8,128)(2,1)S(1)}, bf16[1,64,1024]{2,1,0:T(8,128)(2,1)S(1)}, u32[]{:S(2)}, u32[]{:S(2)}) collective-permute-start(bf16[1,64,1024]{2,1,0:T(8,128)(2,1)S(1)} %dynamic-slice_convert_fusion.10), channel_id=1, source_target_pairs={{0,8},{2,10},{4,12},{6,14},{8,0},{10,2},{12,4},{14,6},{16,24},{18,... | collective-permute-start | bytes 393224 | tf_op jit(solution)/shard_map/ppermute | solution.py:827
  312.4 6.5 %collective-permute-start.10 = (bf16[1,32,1024]{2,1,0:T(8,128)(2,1)S(1)}, bf16[1,32,1024]{2,1,0:T(8,128)(2,1)S(1)}, u32[]{:S(2)}, u32[]{:S(2)}) collective-permute-start(bf16[1,32,1024]{2,1,0:T(8,128)(2,1)S(1)} %dynamic-slice_convert_fusion.11), channel_id=1, source_target_pairs={{0,16},{2,18},{4,20},{6,22},{8,24},{10,26},{12,28},{14,30},{16,0},... | collective-permute-start | bytes 196616 | tf_op jit(solution)/shard_map/ppermute | solution.py:827
  316.0 26.6 %collective-permute-start = (bf16[2,256,768]{2,1,0:T(8,128)(2,1)S(1)}, bf16[2,256,768]{2,1,0:T(8,128)(2,1)S(1)}, u32[]{:S(2)}, u32[]{:S(2)}) collective-permute-start(bf16[2,256,768]{2,1,0:T(8,128)(2,1)S(1)} %dynamic-slice_convert_fusion.2), channel_id=1, source_target_pairs={{0,4},{2,6},{4,0},{6,2},{8,12},{10,14},{12,8},{14,10},{16,20},{18,... | collective-permute-start | bytes 2359304 | tf_op jit(solution)/shard_map/ppermute | solution.py:827
  318.8 23.0 %collective-permute-start.11 = (bf16[1,32,1024]{2,1,0:T(8,128)(2,1)S(1)}, bf16[1,32,1024]{2,1,0:T(8,128)(2,1)S(1)}, u32[]{:S(2)}, u32[]{:S(2)}) collective-permute-start(bf16[1,32,1024]{2,1,0:T(8,128)(2,1)S(1)} %add_convert_fusion.3), channel_id=1, source_target_pairs={{0,16},{2,18},{4,20},{6,22},{8,24},{10,26},{12,28},{14,30},{16,0},... | collective-permute-start | bytes 196616 | tf_op jit(solution)/shard_map/ppermute | solution.py:827
  341.9 79.5 %collective-permute-start.12 = (bf16[1,64,1024]{2,1,0:T(8,128)(2,1)S(1)}, bf16[1,64,1024]{2,1,0:T(8,128)(2,1)S(1)}, u32[]{:S(2)}, u32[]{:S(2)}) collective-permute-start(bf16[1,64,1024]{2,1,0:T(8,128)(2,1)S(1)} %maximum_select_fusion.24), channel_id=1, source_target_pairs={{0,8},{2,10},{4,12},{6,14},{8,0},{10,2},{12,4},{14,6},{16,24},{18,... | collective-permute-start | bytes 393224 | tf_op jit(solution)/shard_map/ppermute | solution.py:827
  344.7 12.1 %collective-permute-start.1 = (bf16[2,128,768]{2,1,0:T(8,128)(2,1)S(1)}, bf16[2,128,768]{2,1,0:T(8,128)(2,1)S(1)}, u32[]{:S(2)}, u32[]{:S(2)}) collective-permute-start(bf16[2,128,768]{2,1,0:T(8,128)(2,1)S(1)} %dynamic-slice_convert_fusion.5), channel_id=1, source_target_pairs={{0,8},{2,10},{4,12},{6,14},{8,0},{10,2},{12,4},{14,6},{16,24},{18,... | collective-permute-start | bytes 1179656 | tf_op jit(solution)/shard_map/ppermute | solution.py:827
  347.7 24.5 %collective-permute-start.24 = (bf16[1,256,1024]{2,1,0:T(8,128)(2,1)S(1)}, bf16[1,256,1024]{2,1,0:T(8,128)(2,1)S(1)}, u32[]{:S(2)}, u32[]{:S(2)}) collective-permute-start(bf16[1,256,1024]{2,1,0:T(8,128)(2,1)S(1)} %dynamic-slice_convert_fusion.3), channel_id=1, source_target_pairs={{0,8},{2,10},{4,12},{6,14},{8,0},{10,2},{12,4},{14,6},{16,24},{18,... | collective-permute-start | bytes 1572872 | tf_op jit(solution)/shard_map/ppermute | solution.py:827
  356.9 13.8 %collective-permute-start.2 = (bf16[2,64,768]{2,1,0:T(8,128)(2,1)S(1)}, bf16[2,64,768]{2,1,0:T(8,128)(2,1)S(1)}, u32[]{:S(2)}, u32[]{:S(2)}) collective-permute-start(bf16[2,64,768]{2,1,0:T(8,128)(2,1)S(1)} %dynamic-slice_convert_fusion.9), channel_id=1, source_target_pairs={{0,16},{2,18},{4,20},{6,22},{8,24},{10,26},{12,28},{14,30},{16,0},... | collective-permute-start | bytes 589832 | tf_op jit(solution)/shard_map/ppermute | solution.py:827
  360.8 27.2 %collective-permute-start.16 = (bf16[2,128,1024]{2,1,0:T(8,128)(2,1)S(1)}, bf16[2,128,1024]{2,1,0:T(8,128)(2,1)S(1)}, u32[]{:S(2)}, u32[]{:S(2)}) collective-permute-start(bf16[2,128,1024]{2,1,0:T(8,128)(2,1)S(1)} %dynamic-slice_convert_fusion.4), channel_id=1, source_target_pairs={{0,8},{2,10},{4,12},{6,14},{8,0},{10,2},{12,4},{14,6},{16,24},{18,... | collective-permute-start | bytes 1572872 | tf_op jit(solution)/shard_map/ppermute | solution.py:827
  370.8 20.6 %collective-permute-start.3 = (bf16[1,64,768]{2,1,0:T(8,128)(2,1)S(1)}, bf16[1,64,768]{2,1,0:T(8,128)(2,1)S(1)}, u32[]{:S(2)}, u32[]{:S(2)}) collective-permute-start(bf16[1,64,768]{2,1,0:T(8,128)(2,1)S(1)} %get-tuple-element.67), channel_id=1, source_target_pairs={{0,1},{1,0},{2,3},{3,2},{4,5},{5,4},{6,7},{7,6},{8,9},{9,8},{10,11... | collective-permute-start | bytes 294920 | tf_op jit(solution)/shard_map/ppermute | solution.py:854
  372.4 16.2 %collective-permute-start.25 = (bf16[1,128,1024]{2,1,0:T(8,128)(2,1)S(1)}, bf16[1,128,1024]{2,1,0:T(8,128)(2,1)S(1)}, u32[]{:S(2)}, u32[]{:S(2)}) collective-permute-start(bf16[1,128,1024]{2,1,0:T(8,128)(2,1)S(1)} %dynamic-slice_convert_fusion.6), channel_id=1, source_target_pairs={{0,16},{2,18},{4,20},{6,22},{8,24},{10,26},{12,28},{14,30},{16,0},... | collective-permute-start | bytes 786440 | tf_op jit(solution)/shard_map/ppermute | solution.py:827
  388.3 23.1 %collective-permute-start.17 = (bf16[2,64,1024]{2,1,0:T(8,128)(2,1)S(1)}, bf16[2,64,1024]{2,1,0:T(8,128)(2,1)S(1)}, u32[]{:S(2)}, u32[]{:S(2)}) collective-permute-start(bf16[2,64,1024]{2,1,0:T(8,128)(2,1)S(1)} %dynamic-slice_convert_fusion.7), channel_id=1, source_target_pairs={{0,16},{2,18},{4,20},{6,22},{8,24},{10,26},{12,28},{14,30},{16,0},... | collective-permute-start | bytes 786440 | tf_op jit(solution)/shard_map/ppermute | solution.py:827
  388.7 28.3 %collective-permute-start.26 = (bf16[1,128,1024]{2,1,0:T(8,128)(2,1)S(1)}, bf16[1,128,1024]{2,1,0:T(8,128)(2,1)S(1)}, u32[]{:S(2)}, u32[]{:S(2)}) collective-permute-start(bf16[1,128,1024]{2,1,0:T(8,128)(2,1)S(1)} %add_convert_fusion), channel_id=1, source_target_pairs={{0,16},{2,18},{4,20},{6,22},{8,24},{10,26},{12,28},{14,30},{16,0},... | collective-permute-start | bytes 786440 | tf_op jit(solution)/shard_map/ppermute | solution.py:827
  391.4 29.8 %collective-permute-start.4 = (bf16[2,64,768]{2,1,0:T(8,128)(2,1)S(1)}, bf16[2,64,768]{2,1,0:T(8,128)(2,1)S(1)}, u32[]{:S(2)}, u32[]{:S(2)}) collective-permute-start(bf16[2,64,768]{2,1,0:T(8,128)(2,1)S(1)} %maximum_select_fusion.22), channel_id=1, source_target_pairs={{0,16},{2,18},{4,20},{6,22},{8,24},{10,26},{12,28},{14,30},{16,0},... | collective-permute-start | bytes 589832 | tf_op jit(solution)/shard_map/ppermute | solution.py:827
  417.1 20.9 %collective-permute-start.27 = (bf16[1,256,1024]{2,1,0:T(8,128)(2,1)S(1)}, bf16[1,256,1024]{2,1,0:T(8,128)(2,1)S(1)}, u32[]{:S(2)}, u32[]{:S(2)}) collective-permute-start(bf16[1,256,1024]{2,1,0:T(8,128)(2,1)S(1)} %maximum_select_fusion.17), channel_id=1, source_target_pairs={{0,8},{2,10},{4,12},{6,14},{8,0},{10,2},{12,4},{14,6},{16,24},{18,... | collective-permute-start | bytes 1572872 | tf_op jit(solution)/shard_map/ppermute | solution.py:827
  417.2 7.4 %collective-permute-start.18 = (bf16[1,64,1024]{2,1,0:T(8,128)(2,1)S(1)}, bf16[1,64,1024]{2,1,0:T(8,128)(2,1)S(1)}, u32[]{:S(2)}, u32[]{:S(2)}) collective-permute-start(bf16[1,64,1024]{2,1,0:T(8,128)(2,1)S(1)} %get-tuple-element.65), channel_id=1, source_target_pairs={{0,1},{1,0},{2,3},{3,2},{4,5},{5,4},{6,7},{7,6},{8,9},{9,8},{10,11... | collective-permute-start | bytes 393224 | tf_op jit(solution)/shard_map/ppermute | solution.py:854
  421.3 25.1 %collective-permute-start.5 = (bf16[2,128,768]{2,1,0:T(8,128)(2,1)S(1)}, bf16[2,128,768]{2,1,0:T(8,128)(2,1)S(1)}, u32[]{:S(2)}, u32[]{:S(2)}) collective-permute-start(bf16[2,128,768]{2,1,0:T(8,128)(2,1)S(1)} %maximum_select_fusion.18), channel_id=1, source_target_pairs={{0,8},{2,10},{4,12},{6,14},{8,0},{10,2},{12,4},{14,6},{16,24},{18,... | collective-permute-start | bytes 1179656 | tf_op jit(solution)/shard_map/ppermute | solution.py:827
  422.2 94.7 %collective-permute-start.13 = (bf16[1,128,1024]{2,1,0:T(8,128)(2,1)}, bf16[1,128,1024]{2,1,0:T(8,128)(2,1)}, u32[]{:S(2)}, u32[]{:S(2)}) collective-permute-start(bf16[1,128,1024]{2,1,0:T(8,128)(2,1)} %maximum_select_fusion.20), channel_id=1, source_target_pairs={{0,4},{2,6},{4,0},{6,2},{8,12},{10,14},{12,8},{14,10},{16,20},{18,... | collective-permute-start | bytes 786440 | tf_op jit(solution)/shard_map/ppermute | solution.py:827
  424.7 24.6 %collective-permute-start.19 = (bf16[2,64,1024]{2,1,0:T(8,128)(2,1)S(1)}, bf16[2,64,1024]{2,1,0:T(8,128)(2,1)S(1)}, u32[]{:S(2)}, u32[]{:S(2)}) collective-permute-start(bf16[2,64,1024]{2,1,0:T(8,128)(2,1)S(1)} %maximum_select_fusion.21), channel_id=1, source_target_pairs={{0,16},{2,18},{4,20},{6,22},{8,24},{10,26},{12,28},{14,30},{16,0},... | collective-permute-start | bytes 786440 | tf_op jit(solution)/shard_map/ppermute | solution.py:827
  439.5 85.1 %collective-permute-start.28 = (bf16[1,512,1024]{2,1,0:T(8,128)(2,1)}, bf16[1,512,1024]{2,1,0:T(8,128)(2,1)}, u32[]{:S(2)}, u32[]{:S(2)}) collective-permute-start(bf16[1,512,1024]{2,1,0:T(8,128)(2,1)} %maximum_select_fusion.11), channel_id=1, source_target_pairs={{0,4},{2,6},{4,0},{6,2},{8,12},{10,14},{12,8},{14,10},{16,20},{18,... | collective-permute-start | bytes 3145736 | tf_op jit(solution)/shard_map/ppermute | solution.py:827
  446.7 76.0 %collective-permute-start.6 = (bf16[2,256,768]{2,1,0:T(8,128)(2,1)S(1)}, bf16[2,256,768]{2,1,0:T(8,128)(2,1)S(1)}, u32[]{:S(2)}, u32[]{:S(2)}) collective-permute-start(bf16[2,256,768]{2,1,0:T(8,128)(2,1)S(1)} %maximum_select_fusion.12), channel_id=1, source_target_pairs={{0,4},{2,6},{4,0},{6,2},{8,12},{10,14},{12,8},{14,10},{16,20},{18,... | collective-permute-start | bytes 2359304 | tf_op jit(solution)/shard_map/ppermute | solution.py:827
  449.4 69.3 %collective-permute-start.20 = (bf16[2,128,1024]{2,1,0:T(8,128)(2,1)S(1)}, bf16[2,128,1024]{2,1,0:T(8,128)(2,1)}, u32[]{:S(2)}, u32[]{:S(2)}) collective-permute-start(bf16[2,128,1024]{2,1,0:T(8,128)(2,1)S(1)} %maximum_select_fusion.15), channel_id=1, source_target_pairs={{0,8},{2,10},{4,12},{6,14},{8,0},{10,2},{12,4},{14,6},{16,24},{18,... | collective-permute-start | bytes 1572872 | tf_op jit(solution)/shard_map/ppermute | solution.py:827
  518.1 10.8 %collective-permute-start.14 = (bf16[1,1,256,1024]{3,2,1,0:T(8,128)(2,1)S(1)}, bf16[1,1,256,1024]{3,2,1,0:T(8,128)(2,1)S(1)}, u32[]{:S(2)}, u32[]{:S(2)}) collective-permute-start(bf16[1,1,256,1024]{3,2,1,0:T(8,128)(2,1)S(1)} %maximum_select_fusion.14), channel_id=1, source_target_pairs={{0,2},{2,0},{4,6},{6,4},{8,10},{10,8},{12,14},{14,12},{16,18},{18,... | collective-permute-start | bytes 1572872 | tf_op jit(solution)/shard_map/ppermute | solution.py:827
  520.3 26.3 %collective-permute-start.21 = (bf16[2,256,1024]{2,1,0:T(8,128)(2,1)S(1)}, bf16[2,256,1024]{2,1,0:T(8,128)(2,1)}, u32[]{:S(2)}, u32[]{:S(2)}) collective-permute-start(bf16[2,256,1024]{2,1,0:T(8,128)(2,1)S(1)} %maximum_select_fusion.9), channel_id=1, source_target_pairs={{0,4},{2,6},{4,0},{6,2},{8,12},{10,14},{12,8},{14,10},{16,20},{18,... | collective-permute-start | bytes 3145736 | tf_op jit(solution)/shard_map/ppermute | solution.py:827
  524.4 29.3 %collective-permute-start.7 = (bf16[1,2,512,768]{3,2,1,0:T(8,128)(2,1)}, bf16[1,2,512,768]{3,2,1,0:T(8,128)(2,1)}, u32[]{:S(2)}, u32[]{:S(2)}) collective-permute-start(bf16[1,2,512,768]{3,2,1,0:T(8,128)(2,1)} %maximum_select_fusion.6), channel_id=1, source_target_pairs={{0,2},{2,0},{4,6},{6,4},{8,10},{10,8},{12,14},{14,12},{16,18},{18,... | collective-permute-start | bytes 4718600 | tf_op jit(solution)/shard_map/ppermute | solution.py:827
  528.6 54.1 %collective-permute-start.29 = (bf16[1,1,1024,1024]{3,2,1,0:T(8,128)(2,1)}, bf16[1,1,1024,1024]{3,2,1,0:T(8,128)(2,1)}, u32[]{:S(2)}, u32[]{:S(2)}) collective-permute-start(bf16[1,1,1024,1024]{3,2,1,0:T(8,128)(2,1)} %maximum_select_fusion.5), channel_id=1, source_target_pairs={{0,2},{2,0},{4,6},{6,4},{8,10},{10,8},{12,14},{14,12},{16,18},{18,... | collective-permute-start | bytes 6291464 | tf_op jit(solution)/shard_map/ppermute | solution.py:827
  550.5 41.7 %collective-permute-start.22 = (bf16[1,2,512,1024]{3,2,1,0:T(8,128)(2,1)}, bf16[1,2,512,1024]{3,2,1,0:T(8,128)(2,1)}, u32[]{:S(2)}, u32[]{:S(2)}) collective-permute-start(bf16[1,2,512,1024]{3,2,1,0:T(8,128)(2,1)} %maximum_select_fusion.4), channel_id=1, source_target_pairs={{0,2},{2,0},{4,6},{6,4},{8,10},{10,8},{12,14},{14,12},{16,18},{18,... | collective-permute-start | bytes 6291464 | tf_op jit(solution)/shard_map/ppermute | solution.py:827
  (19 other events, 170.7 us)

commit v2 on v1

--- a/solution.py
+++ b/solution.py
@@ -823,43 +823,250 @@
     )(qkv, out, lse, do, seg_col, seg_row)
 
 
-def flip(v, bit):
-    return lax.ppermute(v, "band", [(i, i ^ bit) for i in range(16)])
-
-
-def keep_half(v, bit_value, bit):
-    half = v.shape[1] // 2
-    mine = lax.dynamic_slice_in_dim(v, bit_value * half, half, 1)
-    theirs = lax.dynamic_slice_in_dim(v, (1 - bit_value) * half, half, 1)
-    return mine.astype(F32) + flip(theirs.astype(BF), bit).astype(F32)
-
-
-def join_half(v, bit_value, bit):
-    other = flip(v, bit)
-    return jnp.where(
-        bit_value == 0,
-        jnp.concatenate([v, other], axis=1),
-        jnp.concatenate([other, v], axis=1),
-    )
-
-
-def reduce_columns(v, halves):
+CHUNKS = 12
+SWAPPED = ((4, 8), (9, 12))
+
+
+def wsum_body(part, gg, full, gsum, r1, s1, r2, s2, r3, p3, tmp, g1, g2, g3, ss, rs, ls, gs, gr):
     b, y, z, x, c = place()
-    bits = ((x, 2), (z % 2, 4), (z // 2, 8))
-    for value, bit in bits:
-        v = keep_half(v, value, bit)
-    v = v.astype(BF)
-    if halves:
-        mine = lax.dynamic_slice_in_dim(v, y, 1, 0)
-        theirs = lax.ppermute(lax.dynamic_slice_in_dim(v, 1 - y, 1, 0), "seq", [(0, 1), (1, 0)])
-        v = jnp.where(
-            y == 0, jnp.concatenate([mine, theirs], 0), jnp.concatenate([theirs, mine], 0)
+    others = chips(b, c, y)
+    z0, zb = z % 2, z // 2
+    core, over = (b + 1 - 2 * c, y), (b, 1 - y)
+    px, p0, pb = (b + 2 - 4 * x, y), (b + 4 - 8 * z0, y), (b + 8 - 16 * zb, y)
+    o1 = x * 256
+    o2 = o1 + z0 * 128
+    o3 = o2 + zb * 64
+
+    def rows(start, size):
+        return pl.ds(pl.multiple_of(start, 64), size)
+
+    def remote(src, dst, stage, i, peer):
+        return pltpu.make_async_remote_copy(
+            src_ref=src,
+            dst_ref=dst,
+            send_sem=ss.at[stage, i],
+            recv_sem=rs.at[stage, i],
+            device_id=peer,
+            device_id_type=MESH,
         )
-    for value, bit in reversed(bits):
-        v = join_half(v, value, bit)
-    v = v[None]
-    other = flip(v, 1)
-    return jnp.where(c == 0, jnp.concatenate([v, other], 0), jnp.concatenate([other, v], 0))
+
+    def c_x(i):
+        return remote(part.at[i, :, rows((1 - x) * 256, 256)], r1.at[i], 0, i, px)
+
+    def c_z0(i):
+        return remote(s1.at[i, :, rows((1 - z0) * 128, 128)], r2.at[i], 1, i, p0)
+
+    def c_zb(i):
+        return remote(s2.at[i, :, rows((1 - zb) * 64, 64)], r3.at[i], 2, i, pb)
+
+    def c_y(i):
+        return remote(tmp.at[i], p3.at[i, y], 3, i, over)
+
+    def c_gb(i):
+        return remote(p3.at[i], full.at[i, c, :, rows(o3, 64)], 4, i, pb)
+
+    def c_own(i):
+        return pltpu.make_async_copy(p3.at[i], full.at[i, c, :, rows(o3, 64)], ls.at[i])
+
+    def c_g0(i):
+        src = full.at[i, c, :, rows(o2, 128)]
+        return remote(src, src, 5, i, p0)
+
+    def c_gx(i):
+        src = full.at[i, c, :, rows(o1, 256)]
+        return remote(src, src, 6, i, px)
+
+    def c_core(i):
+        src = full.at[i, c]
+        return remote(src, src, 7, i, core)
+
+    meet([core, over] + [peer for _, peer in others])
+
+    @pl.loop(0, CHUNKS)
+    def _(i):
+        c_x(i).start()
+
+    gcps = [send(gg, g1.at[0], gs.at[0], gr.at[0], core)]
+    gcps[0].wait_recv()
+    g1[1] = g1[0] + gg[...]
+    gcps.append(send(g1.at[1], g2.at[0], gs.at[1], gr.at[1], over))
+    gcps[1].wait_recv()
+    j = b // 2
+    g3[j] = g1[1] + g2[0]
+    for k, (jd, peer) in enumerate(others):
+        gcps.append(send(g3.at[j], g3.at[j], gs.at[2 + k], gr.at[2 + k], peer))
+
+    def when_chunk(t, lag, act, ranges=((0, CHUNKS),)):
+        for lo, hi in ranges:
+
+            @pl.when((t - lag >= lo) & (t - lag < hi))
+            def _():
+                act(t - lag)
+
+    def add_x(i):
+        c_x(i).wait_recv()
+        mine = part[i, :, rows(x * 256, 256)].astype(F32)
+        s1[i] = (mine + r1[i].astype(F32)).astype(BF)
+        c_z0(i).start()
+
+    def add_z0(i):
+        c_z0(i).wait_recv()
+        mine = s1[i, :, rows(z0 * 128, 128)].astype(F32)
+        s2[i] = (mine + r2[i].astype(F32)).astype(BF)
+        c_zb(i).start()
+
+    def add_zb_plain(i):
+        c_zb(i).wait_recv()
+        mine = s2[i, :, rows(zb * 64, 64)].astype(F32)
+        p3[i] = (mine + r3[i].astype(F32)).astype(BF)
+        c_gb(i).start()
+        c_own(i).start()
+
+    def add_zb_swap(i):
+        c_zb(i).wait_recv()
+        for h, dst in ((y, p3.at[i, y]), (1 - y, tmp.at[i])):
+            mine = s2[i, h, rows(zb * 64, 64)].astype(F32)
+            dst[...] = (mine + r3[i, h].astype(F32)).astype(BF)
+        c_y(i).start()
+
+    def take_y(i):
+        c_y(i).wait_recv()
+        c_gb(i).start()
+        c_own(i).start()
+
+    def grow_z0(i):
+        c_gb(i).wait_recv()
+        c_own(i).wait()
+        c_g0(i).start()
+
+    def grow_x(i):
+        c_g0(i).wait_recv()
+        c_gx(i).start()
+
+    def grow_core(i):
+        c_gx(i).wait_recv()
+        c_core(i).start()
+
+    plain = ((0, 4), (8, 9))
+
+    @pl.loop(0, CHUNKS + 6)
+    def _(t):
+        when_chunk(t, 6, grow_core)
+        when_chunk(t, 5, grow_x)
+        when_chunk(t, 4, grow_z0)
+        when_chunk(t, 3, take_y, SWAPPED)
+        when_chunk(t, 2, add_zb_plain, plain)
+        when_chunk(t, 2, add_zb_swap, SWAPPED)
+        when_chunk(t, 1, add_z0)
+        when_chunk(t, 0, add_x)
+
+    @pl.loop(0, CHUNKS)
+    def _(i):
+        c_core(i).wait_recv()
+        for cp in (c_x, c_z0, c_zb, c_gb, c_g0, c_gx, c_core):
+            cp(i).wait_send()
+
+    for lo, hi in SWAPPED:
+
+        @pl.loop(lo, hi)
+        def _(i):
+            c_y(i).wait_send()
+
+    for cp in gcps[:2]:
+        cp.wait_send()
+    for cp in gcps[2:]:
+        cp.wait()
+    total = g3[0]
+    for k in range(1, 8):
+        total = total + g3[k]
+    gsum[...] = total
+
+
+def weight_sums(part, gg):
+    return pl.pallas_call(
+        wsum_body,
+        out_shape=[
+            jax.ShapeDtypeStruct((CHUNKS, 2, 2, 512, 256), BF),
+            jax.ShapeDtypeStruct((8, 1024), F32),
+        ],
+        in_specs=[pl.BlockSpec(memory_space=pltpu.VMEM)] * 2,
+        out_specs=[pl.BlockSpec(memory_space=pl.ANY), pl.BlockSpec(memory_space=pltpu.VMEM)],
+        scratch_shapes=[
+            pltpu.VMEM((CHUNKS, 2, 256, 256), BF),
+            pltpu.VMEM((CHUNKS, 2, 256, 256), BF),
+            pltpu.VMEM((CHUNKS, 2, 128, 256), BF),
+            pltpu.VMEM((CHUNKS, 2, 128, 256), BF),
+            pltpu.VMEM((CHUNKS, 2, 64, 256), BF),
+            pltpu.VMEM((CHUNKS, 2, 64, 256), BF),
+            pltpu.VMEM((CHUNKS, 64, 256), BF),
+            pltpu.VMEM((2, 8, 1024), F32),
+            pltpu.VMEM((1, 8, 1024), F32),
+            pltpu.VMEM((8, 8, 1024), F32),
+            pltpu.SemaphoreType.DMA((8, CHUNKS)),
+            pltpu.SemaphoreType.DMA((8, CHUNKS)),
+            pltpu.SemaphoreType.DMA((CHUNKS,)),
+            dma(9),
+            dma(9),
+        ],
+        compiler_params=pltpu.CompilerParams(collective_id=9, has_side_effects=True),
+        name="weight_sums",
+    )(part, gg)
+
+
+def widen_body(src, dst):
+    for k in range(4):
+        dst[:, k * 256 : k * 256 + 256] = src[k].astype(F32)
+
+
+def widen_out_body(src, dst):
+    for h in range(2):
+        for k in range(2):
+            col = (h * 2 + k) * 256
+            dst[:, col : col + 256] = src[h, k * 256 : k * 256 + 256].astype(F32)
+
+
+def widen_qkv_body(src, dst):
+    for r in range(4):
+        for t in range(6):
+            col = (t % 3) * 1024 + r * 256 + (t // 3) * 128
+            half = (t % 2) * 128
+            dst[:, col : col + 128] = src[t // 2, r % 2, r // 2, :, half : half + 128].astype(F32)
+
+
+def widen_all(full):
+    down = pl.pallas_call(
+        widen_body,
+        grid=(4,),
+        in_specs=[pl.BlockSpec((4, None, None, 512, 256), lambda r: (0, r // 2, r % 2, 0, 0))],
+        out_specs=pl.BlockSpec((512, 1024), lambda r: (r, 0)),
+        out_shape=jax.ShapeDtypeStruct((2048, 1024), F32),
+        name="widen_down",
+    )(full)
+    up = pl.pallas_call(
+        widen_body,
+        grid=(4,),
+        in_specs=[pl.BlockSpec((4, None, None, 512, 256), lambda r: (1, r % 2, r // 2, 0, 0))],
+        out_specs=pl.BlockSpec((512, 1024), lambda r: (0, r)),
+        out_shape=jax.ShapeDtypeStruct((512, 4096), F32),
+        name="widen_up",
+    )(full)
+    out = pl.pallas_call(
+        widen_out_body,
+        grid=(2,),
+        in_specs=[pl.BlockSpec((None, None, 2, 512, 256), lambda r: (8, r, 0, 0, 0))],
+        out_specs=pl.BlockSpec((256, 1024), lambda r: (r, 0)),
+        out_shape=jax.ShapeDtypeStruct((512, 1024), F32),
+        name="widen_out",
+    )(full)
+    qkv = pl.pallas_call(
+        widen_qkv_body,
+        grid=(4,),
+        in_specs=[pl.BlockSpec((3, 2, 2, 128, 256), lambda i: (3, 0, 0, i, 0))],
+        out_specs=pl.BlockSpec((128, 3072), lambda i: (i, 0)),
+        out_shape=jax.ShapeDtypeStruct((512, 3072), F32),
+        name="widen_qkv",
+    )(full)
+    return down, up, out, qkv
 
 
 def column_device(
@@ -919,31 +1126,38 @@
     )
     down_grad = first_dot(hidden_low, grad_two)
     up_grad = first_dot(h_two, pre_grad)
-    down_sum = reduce_columns(down_grad.reshape(1, 1024, 1024), False)
-    up_sum = reduce_columns(up_grad.reshape(2, 512, 1024), True)
     attn_grad = last_dot(branch, out_rows).astype(BF)
     do, layer_out = grad_heads(
         attn_grad.reshape(4, 192, 256), branch_two.reshape(4, 2, 96, 1024), resid, valid
     )
     outproj_grad = first_dot(attn_low, branch)
-    out_sum = reduce_columns(outproj_grad.reshape(1, 256, 1024), False)
     dqkv = attend_back(att, out_full, lse, do.reshape(1536, 128), seg_col, seg_row)
     dqkv_rows = grad_rows(dqkv.reshape(8, 192, 384)).reshape(768, 768)
     c_part = last_dot(dqkv_rows, w_sel).astype(BF)
     token_grad, gain_one_grad = first_back(c_part.reshape(4, 2, 96, 1024), tokens, rgrad, gain)
     qkv_grad = first_dot(h_one, dqkv_rows)
-    qkv_sum = reduce_columns(qkv_grad.reshape(2, 512, 768), True)
-    both = lax.psum(jnp.stack([gain_one_grad[0], gain_two_grad[0]]), ("band", "seq"))
-    gain_out = lax.dynamic_slice_in_dim(both, y * 512, 512, 1)
-    qkv_out = jnp.transpose(qkv_sum.reshape(2, 2, 512, 2, 3, 128), (2, 4, 1, 0, 3, 5))
-    up_out = jnp.transpose(up_sum, (2, 1, 0, 3))
+    part = jnp.concatenate(
+        [
+            jnp.transpose(down_grad.astype(BF).reshape(2, 512, 4, 256), (2, 0, 1, 3)),
+            jnp.transpose(up_grad.astype(BF).reshape(2, 512, 4, 256), (2, 0, 1, 3)),
+            jnp.transpose(outproj_grad.astype(BF).reshape(256, 4, 256), (1, 0, 2)).reshape(
+                1, 2, 512, 256
+            ),
+            jnp.transpose(qkv_grad.astype(BF).reshape(2, 512, 3, 256), (2, 0, 1, 3)),
+        ],
+        0,
+    )
+    rows8 = lax.broadcasted_iota(jnp.int32, (8, 1024), 0)
+    full, gain_sum = weight_sums(part, jnp.where(rows8 == 0, gain_one_grad, gain_two_grad))
+    down_out, up_out, out_out, qkv_out = widen_all(full)
+    gain_out = lax.dynamic_slice_in_dim(gain_sum, y * 512, 512, 1)
     return (
         layer_out,
         token_grad,
-        qkv_out.reshape(512, 3072).astype(F32),
-        out_sum.reshape(512, 1024).astype(F32),
-        up_out.reshape(512, 4096).astype(F32),
-        down_sum.reshape(2048, 1024).astype(F32),
+        qkv_out,
+        out_out,
+        up_out,
+        down_out,
         gain_out[0],
         gain_out[1],
     )

time: 624 us -> 510 us (0.82)
  Pallas kernels: 242 us -> 424 us
  waiting for transfers between devices: 83.4 us -> 0 us
  blocking collectives: 65.6 us -> 0 us
  other arithmetic: 66.9 us -> 13.8 us
  starting transfers between devices: 41.5 us -> 0 us
  local copies, waits for them, and re-layouts: 67.6 us -> 26.7 us
  matrix products: 50.9 us -> 43.8 us
    pallas_call x0 -> x5, Pallas kernels: none -> 197 us  [the longest x1 178 us: weight_sums(): pl.pallas_call(wsum_body, out_shape=[jax.ShapeDtypeStruct((CHUNKS, 2, 2,...]
    ppermute x30 -> x0, waiting for transfers between devices: 83.4 us -> none  [the longest x28 83.4 us: flip(): return lax.ppermute(v, 'band', [(i, i ^ bit) for i in range(16)])]
    psum x1 -> x0, blocking collectives: 65.6 us -> none  [column_device(): lax.psum(jnp.stack([gain_one_grad[0], gain_two_grad[0]]), ('band', 'seq'))]
    ppermute x30 -> x0, starting transfers between devices: 41.5 us -> none  [the longest x28 40.1 us: flip(): return lax.ppermute(v, 'band', [(i, i ^ bit) for i in range(16)])]
    convert_element_type x14 -> x0, local copies, waits for them, and re-layouts: 26.9 us -> none  [the longest x12 9.19 us: keep_half(): return mine.astype(F32) + flip(theirs.astype(BF), bit).astype(F32)]
    select_n x20 -> x1, other arithmetic: 25.1 us -> 1.45 us  [column_device(): jnp.where(rows8 == 0, gain_one_grad, gain_two_grad)]
    convert_element_type x8 -> x0, other arithmetic: 21.8 us -> none  [the longest x1 7.76 us: column_device(): qkv_out.reshape(512, 3072).astype(F32)]
    unnamed x46 -> x40, local copies, waits for them, and re-layouts: 18.2 us -> 3.07 us
  transfers between devices with their start and end apart: 30 -> 0, of which waited for: 10 -> 0; matrix products, arithmetic and copies ran while one was open for 19% -> 0% of each run, Pallas kernels for 14% -> 0%
where the time goes in v2:
time: 510 us; the launch traced here: 509 us
  Pallas kernels  424 us (83%)
  matrix products  43.8 us (9%)
  local copies, waits for them, and re-layouts  26.7 us (5%)
  other arithmetic  13.8 us (3%)
    pallas_call x1, Pallas kernels, weight_sums(): pl.pallas_call(wsum_body, out_shape=[jax.ShapeDtypeStruct((CHUNKS, 2, 2,...  178 us
    pallas_call x1, Pallas kernels, open_call(): comm_call(open_body, 'open_column', 1, [((4, 2, 96, 1024), BF), ((2, 2, 1...  34.2 us
    pallas_call x1, Pallas kernels, to_heads(): comm_call(to_heads_body, 'to_heads', 2, [((8, 192, 384), BF), ((2, 512, 1...  32.1 us
    pallas_call x1, Pallas kernels, second_norm(): comm_call(second_norm_body, 'second_norm', 4, [((2, 96, 1024), F32), ((4,...  28.5 us
    pallas_call x1, Pallas kernels, second_back(): comm_call(second_back_body, 'second_back', 5, [((2, 96, 1024), F32), ((8,...  27.4 us
    pallas_call x1, Pallas kernels, grad_rows(): comm_call(grad_rows_body, 'grad_rows', 7, [((4, 192, 768), BF)], [dma(7),...  23.8 us
    dot_general x4, matrix products, plain_dot(): lax.dot_general(a, b, (((1,), (0,)), ((), ())), preferred_element_type=F32)  18.1 us
    pallas_call x1, Pallas kernels, grad_heads(): comm_call(grad_heads_body, 'grad_heads', 6, [((8, 192, 128), BF), ((2, 96...  17.9 us

profile of v2, /device:TPU:0, one launch (start us, length us, event | category | flops | bytes accessed | tf_op | source)
XLA Modules:
  0.0 509.1 jit_solution(15131836463267681369)
XLA Ops:
  4.3 34.2 %open_column.1 = (bf16[4,2,96,1024]{3,2,1,0:T(8,128)(2,1)}, s32[2,2,1536]{2,1,0:T(2,128)}, bf16[2,512,768]{2,1,0:T(8,128)(2,1)}, f32[2,8,512]{2,1,0:T(8,128)}) custom-call(bf16[2,96,1024]{2,1,0:T(8,128)(2,1)} %tok.5, s32[2,1536]{1,0:T(2,128)} %seg.1, bf16[512,3072]{1,0:T(8,128)(2,1)} %wqkv.1, f32[8,512]{1,0:T(8,128)} %fusion.32.gains), custom_call_target="tpu_custom_call" | custom-call | tf_op jit(solution)/shard_map/open_column/pallas_call | solution.py:426
  42.0 2.1 fusion.2
  46.5 2.4 convolution_convert_fusion.6
  49.0 32.1 %to_heads.1 = (bf16[8,192,384]{2,1,0:T(8,128)(2,1)}, bf16[2,512,1024]{2,1,0:T(8,128)(2,1)}) custom-call(bf16[4,192,768]{2,1,0:T(8,128)(2,1)} %bitcast.73, bf16[512,4096]{1,0:T(8,128)(2,1)} %up.1), custom_call_target="tpu_custom_call" | custom-call | tf_op jit(solution)/shard_map/to_heads/pallas_call | solution.py:467
  81.0 12.6 %attend.1 = (bf16[1536,128]{1,0:T(8,128)(2,1)}, f32[1536,128]{1,0:T(8,128)}, f32[1536,128]{1,0:T(8,128)}) custom-call(bf16[1536,384]{1,0:T(8,128)(2,1)} %bitcast.62, s32[1536,128]{1,0:T(8,128)} %broadcast_in_dim.9.seg_col, s32[8,1536]{1,0:T(8,128)} %broadcast_in_dim.10.seg_row), custom_call_target="tpu_custom_call" | custom-call | tf_op jit(solution)/shard_map/attend/pallas_call | solution.py:737
  93.6 17.6 %from_heads.1 = (bf16[4,192,256]{2,1,0:T(8,128)(2,1)}, bf16[4,2,96,1024]{3,2,1,0:T(8,128)(2,1)}) custom-call(bf16[8,192,128]{2,1,0:T(8,128)(2,1)} %bitcast.76, bf16[2,96,1024]{2,1,0:T(8,128)(2,1)} %cot.3), custom_call_target="tpu_custom_call" | custom-call | tf_op jit(solution)/shard_map/from_heads/pallas_call | solution.py:509
  114.8 28.5 %second_norm.1 = (f32[2,96,1024]{2,1,0:T(8,128)}, bf16[4,2,96,1024]{3,2,1,0:T(8,128)(2,1)}) custom-call(bf16[4,2,96,1024]{3,2,1,0:T(8,128)(2,1)} %bitcast.61, bf16[2,96,1024]{2,1,0:T(8,128)(2,1)} %tok.5, f32[2,96,128]{2,1,0:T(8,128)} %broadcast_in_dim.11.valid, f32[8,1024]{1,0:T(8,128)} %bitcast.81), custom_call_target="tpu_custom_call" | custom-call | tf_op jit(solution)/shard_map/second_norm/pallas_call | solution.py:585
  143.3 11.0 %fusion.12 = (bf16[768,1024]{1,0:T(8,128)(2,1)}, f32[768,1024]{1,0:T(8,128)S(1)}) fusion(bf16[768,1024]{1,0:T(8,128)(2,1)} %bitcast.91, bf16[1024,1024]{1,0:T(8,128)(2,1)} %bitcast.87), kind=kOutput, calls=%fused_computation.17 | convolution fusion | flops 1661730816 | bytes 8388608 | tf_op jit(solution)/shard_map/dot_general | solution.py:706
  154.3 3.0 fusion.9
  157.3 3.0 convolution_convert_fusion.4
  160.3 3.2 convolution_convert_fusion
  163.5 3.3 reshape.170
  166.9 5.2 %convolution_convert_fusion.1 = bf16[1024,1024]{1,0:T(8,128)(2,1)} fusion(bf16[768,1024]{1,0:T(8,128)(2,1)} %get-tuple-element.54, bf16[768,1024]{1,0:T(8,128)(2,1)} %copy-done.6), kind=kOutput, calls=%fused_computation.38 | convolution fusion | flops 1611661312 | bytes 5242880 | tf_op jit(solution)/shard_map/dot_general | solution.py:1124
  172.0 3.0 fusion.24
  175.0 4.5 reshape.169
  179.5 4.2 copy_bitcast_fusion
  183.8 27.4 %second_back.1 = (f32[2,96,1024]{2,1,0:T(8,128)}, f32[8,1024]{1,0:T(8,128)}, bf16[4,2,96,1024]{3,2,1,0:T(8,128)(2,1)}) custom-call(bf16[4,2,96,1024]{3,2,1,0:T(8,128)(2,1)} %bitcast.69, f32[2,96,1024]{2,1,0:T(8,128)} %get-tuple-element.40.resid, bf16[2,96,1024]{2,1,0:T(8,128)(2,1)} %cot.3, f32[2,96,128]{2,1,0:T(8,128)} %broadcast_in_dim.11.valid, ...), custom_call_target="tpu_custom_call" | custom-call | tf_op jit(solution)/shard_map/second_back/pallas_call | solution.py:615
  211.2 2.0 convolution_convert_fusion.7
  213.2 2.8 convolution_convert_fusion.8
  216.0 17.9 %grad_heads.1 = (bf16[8,192,128]{2,1,0:T(8,128)(2,1)}, bf16[2,96,1024]{2,1,0:T(8,128)(2,1)}) custom-call(bf16[4,192,256]{2,1,0:T(8,128)(2,1)} %bitcast.79, bf16[4,2,96,1024]{3,2,1,0:T(8,128)(2,1)} %bitcast.68, f32[2,96,1024]{2,1,0:T(8,128)} %get-tuple-element.40.resid, f32[2,96,128]{2,1,0:T(8,128)} %broadcast_in_dim.11.valid), custom_call_target="tpu_custom_call" | custom-call | tf_op jit(solution)/shard_map/grad_heads/pallas_call | solution.py:645
  233.9 17.5 %attend_back.1 = bf16[1536,384]{1,0:T(8,128)(2,1)} custom-call(bf16[1536,384]{1,0:T(8,128)(2,1)} %bitcast.63, f32[1536,128]{1,0:T(8,128)} %get-tuple-element.43.out, f32[1536,128]{1,0:T(8,128)} %get-tuple-element.44.lse, bf16[1536,128]{1,0:T(8,128)(2,1)} %bitcast.75, s32[1536,128]{1,0:T(8,128)} %broadcast_in_dim.9.seg_col, s32[8,1536]{1,0:T(8,128)} %broadcast_in_dim.10.seg_row), custom_call_target="tpu_custom_call" | custom-call | tf_op jit(solution)/shard_map/attend_back/pallas_call | solution.py:803
  251.5 23.8 %grad_rows.1 = bf16[4,192,768]{2,1,0:T(8,128)(2,1)} custom-call(bf16[8,192,384]{2,1,0:T(8,128)(2,1)} %bitcast.64), custom_call_target="tpu_custom_call" | custom-call | tf_op jit(solution)/shard_map/grad_rows/pallas_call | solution.py:669
  275.3 4.0 convolution_convert_fusion.2
  279.3 2.6 convolution_convert_fusion.3
  281.9 14.8 %first_back.1 = (f32[2,96,1024]{2,1,0:T(8,128)}, f32[8,1024]{1,0:T(8,128)}) custom-call(bf16[4,2,96,1024]{3,2,1,0:T(8,128)(2,1)} %bitcast.70, bf16[2,96,1024]{2,1,0:T(8,128)(2,1)} %tok.5, f32[2,96,1024]{2,1,0:T(8,128)} %get-tuple-element.46.rgrad, f32[8,1024]{1,0:T(8,128)} %bitcast.83), custom_call_target="tpu_custom_call" | custom-call | tf_op jit(solution)/shard_map/first_back/pallas_call | solution.py:691
  298.2 4.2 reshape.176
  304.0 4.7 pad_maximum_fusion.part
  308.6 177.6 %weight_sums.1 = (bf16[12,2,2,512,256]{4,3,2,1,0:T(8,128)(2,1)}, f32[8,1024]{1,0:T(8,128)}) custom-call(bf16[12,2,512,256]{3,2,1,0:T(8,128)(2,1)} %pad_maximum_fusion.part, f32[8,1024]{1,0:T(8,128)} %broadcast_select_fusion.gg), custom_call_target="tpu_custom_call" | custom-call | tf_op jit(solution)/shard_map/weight_sums/pallas_call | solution.py:986
  487.7 2.4 widen_out.1
  490.1 5.2 %widen_qkv.1 = f32[512,3072]{1,0:T(8,128)} custom-call(bf16[12,2,2,512,256]{4,3,2,1,0:T(8,128)(2,1)} %get-tuple-element.50.src), custom_call_target="tpu_custom_call" | custom-call | tf_op jit(solution)/shard_map/widen_qkv/pallas_call | solution.py:1061
  495.3 6.0 %widen_down.1 = f32[2048,1024]{1,0:T(8,128)} custom-call(bf16[12,2,2,512,256]{4,3,2,1,0:T(8,128)(2,1)} %get-tuple-element.50.src), custom_call_target="tpu_custom_call" | custom-call | tf_op jit(solution)/shard_map/widen_down/pallas_call | solution.py:1037
  501.3 6.1 %widen_up.1 = f32[512,4096]{1,0:T(8,128)} custom-call(bf16[12,2,2,512,256]{4,3,2,1,0:T(8,128)(2,1)} %get-tuple-element.50.src), custom_call_target="tpu_custom_call" | custom-call | tf_op jit(solution)/shard_map/widen_up/pallas_call | solution.py:1045
  (63 shorter events, 19.2 us)
Async XLA Ops:
  0.6 112.4 %copy-start = (bf16[512,1024]{1,0:T(8,128)(2,1)S(1)}, bf16[512,1024]{1,0:T(8,128)(2,1)}, u32[]{:S(2)}) copy-start(bf16[512,1024]{1,0:T(8,128)(2,1)} %param.12) | copy-start | bytes 3145732
  38.4 5.7 %copy-start.2 = (bf16[4,2,96,1024]{3,2,1,0:T(8,128)(2,1)S(1)}, bf16[4,2,96,1024]{3,2,1,0:T(8,128)(2,1)}, u32[]{:S(2)}) copy-start(bf16[4,2,96,1024]{3,2,1,0:T(8,128)(2,1)} %get-tuple-element.31) | copy-start | bytes 4718596
  42.0 4.5 copy-start.15
  44.7 4.3 copy-start.4
  111.2 1.8 copy-start.10
  113.0 41.3 %copy-start.6 = (bf16[768,1024]{1,0:T(8,128)(2,1)}, bf16[768,1024]{1,0:T(8,128)(2,1)S(1)}, u32[]{:S(2)}) copy-start(bf16[768,1024]{1,0:T(8,128)(2,1)S(1)} %fusion.13) | copy-start | bytes 4718596
  143.2 11.0 %copy-start.12 = (bf16[2048,1024]{1,0:T(8,128)(2,1)S(1)}, bf16[2048,1024]{1,0:T(8,128)(2,1)}, u32[]{:S(2)}) copy-start(bf16[2048,1024]{1,0:T(8,128)(2,1)} %param.14) | copy-start | bytes 12582916
  154.3 3.0 copy-start.14
  157.3 3.0 copy-start.17
  166.8 5.2 %copy-start.13 = (bf16[2048,1024]{1,0:T(8,128)(2,1)S(1)}, bf16[2048,1024]{1,0:T(8,128)(2,1)}, u32[]{:S(2)}) copy-start(bf16[2048,1024]{1,0:T(8,128)(2,1)} %param.14) | copy-start | bytes 12582916
  166.8 5.2 %copy-start.18 = (bf16[768,1024]{1,0:T(8,128)(2,1)S(1)}, bf16[768,1024]{1,0:T(8,128)(2,1)}, u32[]{:S(2)}) copy-start(bf16[768,1024]{1,0:T(8,128)(2,1)} %get-tuple-element.54) | copy-start | bytes 4718596
  233.9 41.4 %copy-start.5 = (bf16[4,2,96,1024]{3,2,1,0:T(8,128)(2,1)S(1)}, bf16[4,2,96,1024]{3,2,1,0:T(8,128)(2,1)}, u32[]{:S(2)}) copy-start(bf16[4,2,96,1024]{3,2,1,0:T(8,128)(2,1)} %copy-done.4) | copy-start | bytes 4718596
  275.3 4.0 copy-start.7
  275.3 4.0 copy-start.16
  279.3 17.4 %copy-start.11 = (f32[8,1024]{1,0:T(8,128)S(1)}, f32[8,1024]{1,0:T(8,128)}, u32[]{:S(2)}) copy-start(f32[8,1024]{1,0:T(8,128)} %get-tuple-element.49) | copy-start | bytes 98308
  302.4 1.6 copy-start.3
  501.3 6.1 %copy-start.9 = (bf16[2,96,1024]{2,1,0:T(8,128)(2,1)S(1)}, bf16[2,96,1024]{2,1,0:T(8,128)(2,1)}, u32[]{:S(2)}) copy-start(bf16[2,96,1024]{2,1,0:T(8,128)(2,1)} %get-tuple-element.66) | copy-start | bytes 1179652
  501.3 6.9 %copy-start.8 = (f32[2,96,1024]{2,1,0:T(8,128)S(1)}, f32[2,96,1024]{2,1,0:T(8,128)}, u32[]{:S(2)}) copy-start(f32[2,96,1024]{2,1,0:T(8,128)} %get-tuple-element.67) | copy-start | bytes 2359300
  501.3 7.8 %copy-start.1 = (bf16[512,1024]{1,0:T(8,128)(2,1)S(1)}, bf16[512,1024]{1,0:T(8,128)(2,1)}, u32[]{:S(2)}) copy-start(bf16[512,1024]{1,0:T(8,128)(2,1)} %param.12) | copy-start | bytes 3145732

commit v3 on v2

--- a/solution.py
+++ b/solution.py
@@ -474,48 +474,6 @@
     )(qkv, up)
 
 
-def from_heads_body(attn, cot, rows, cot_all, ss, rs):
-    b, y, z, x, c = place()
-    core, over = (b + 1 - 2 * c, y), (b, 1 - y)
-    others = chips(b, c, y)
-    meet([core, over] + [peer for _, peer in others])
-    col = pl.multiple_of(x * 128, 128)
-    cps, side = [], []
-    for k, (jd, peer) in enumerate(others):
-        cps.append(send(attn.at[jd], rows.at[z, :, pl.ds(col, 128)], ss.at[k], rs.at[k], peer))
-    k = 7
-    near = []
-    for m in range(2):
-        near.append(send(cot.at[m], cot_all.at[2 * y + m, c], ss.at[k], rs.at[k], over))
-        k += 1
-    for m in range(2):
-        side.append(send(cot.at[m], cot_all.at[2 * y + m, c], ss.at[k], rs.at[k], core))
-        k += 1
-    rows[z, :, pl.ds(col, 128)] = attn[b // 2]
-    for m in range(2):
-        cot_all[2 * y + m, c] = cot[m]
-    for m in range(2):
-        near[m].wait_recv()
-        got = cot_all.at[2 * (1 - y) + m, c]
-        side.append(send(got, got, ss.at[k], rs.at[k], core))
-        k += 1
-    for cp in near:
-        cp.wait_send()
-    for cp in cps + side:
-        cp.wait()
-
-
-def from_heads(attn, cot):
-    return comm_call(
-        from_heads_body,
-        "from_heads",
-        3,
-        [((4, 192, 256), BF), ((4, 2, 96, 1024), BF)],
-        [dma(13), dma(13)],
-        2,
-    )(attn, cot)
-
-
 def column_sum(part, got, mid, fin, ss, rs, b, y, c):
     core, over = (b + 1 - 2 * c, y), (b, 1 - y)
     first = []
@@ -569,87 +527,306 @@
 ]
 
 
-def second_norm_body(part, tok, valid, gain, resid, h_all, got, mid, fin, own, ss, rs):
+def first_dot(a, d):
+    return lax.dot_general(a, d, (((0,), (0,)), ((), ())), preferred_element_type=F32)
+
+
+def middle_body(
+    att,
+    cot,
+    tok,
+    valid,
+    valid_all,
+    gain,
+    out_w,
+    up_w,
+    down_w,
+    do,
+    layer_out,
+    rgrad,
+    ggrad,
+    part,
+    rows,
+    cot_all,
+    h_all,
+    b_all,
+    buf,
+    gots,
+    mids,
+    fins,
+    own,
+    grad_two,
+    hgrad,
+    hidden,
+    pgrad,
+    agrad,
+    resid,
+    a_s,
+    a_r,
+    c_s,
+    c_r,
+    r_s,
+    r_r,
+    s_s,
+    s_r,
+    d_s,
+    d_r,
+):
     b, y, z, x, c = place()
-    meet([(b + 1 - 2 * c, y), (b, 1 - y)])
-    sums = column_sum(part, got, mid, fin, ss, rs, b, y, c)
-    for m in range(2):
-        res = tok[m].astype(F32) + valid[m][:, :1] * sums[m]
+    core, over = (b + 1 - 2 * c, y), (b, 1 - y)
+    j = b // 2
+    others = chips(b, c, y)
+    mine = pl.ds(pl.multiple_of(c * 96, 32), 96)
+    theirs = pl.ds(pl.multiple_of((1 - c) * 96, 32), 96)
+    far = [2 * (1 - y) + m for m in range(2)]
+    near = [2 * y + m for m in range(2)]
+    col = pl.multiple_of(x * 128, 128)
+    meet([core, over] + [peer for _, peer in others])
+
+    def sum_start(k, q, i):
+        return send(buf.at[k, q, theirs], gots.at[k, q], r_s.at[k, i], r_r.at[k, i], core)
+
+    def sum_over(k, m, first):
+        first.wait_recv()
+        q = far[m]
+        mids[k, m] = (buf[k, q, mine].astype(F32) + gots[k, q].astype(F32)).astype(BF)
+        return send(mids.at[k, m], fins.at[k, m], r_s.at[k, 4 + m], r_r.at[k, 4 + m], over)
+
+    def sum_end(k, m, first, second):
+        first.wait_recv()
+        second.wait_recv()
+        q = near[m]
+        return buf[k, q, mine].astype(F32) + gots[k, q].astype(F32) + fins[k, m].astype(F32)
+
+    def spread_start(k, m, full):
+        to = full.at[near[m], mine]
+        full[near[m], mine] = own[k, m]
+        return (
+            send(own.at[k, m], to, s_s.at[k, m], s_r.at[k, m], over),
+            send(own.at[k, m], to, s_s.at[k, 2 + m], s_r.at[k, 2 + m], core),
+        )
+
+    def spread_pass(k, m, full, pair):
+        pair[0].wait_recv()
+        got = full.at[far[m], mine]
+        return send(got, got, s_s.at[k, 4 + m], s_r.at[k, 4 + m], core)
+
+    done = []
+    for k, (jd, peer) in enumerate(others):
+        done.append(send(att.at[jd], rows.at[z, :, pl.ds(col, 128)], a_s.at[k], a_r.at[k], peer))
+    cots = []
+    for m in range(2):
+        to = cot_all.at[near[m], mine]
+        cots.append(send(cot.at[m], to, c_s.at[m], c_r.at[m], over))
+    for m in range(2):
+        to = cot_all.at[near[m], mine]
+        cots.append(send(cot.at[m], to, c_s.at[2 + m], c_r.at[2 + m], core))
+        cot_all[near[m], mine] = cot[m]
+    rows[z, :, pl.ds(col, 128)] = att[j]
+    for cp in done:
+        cp.wait_recv()
+
+    out_rows = out_w[pl.ds(pl.multiple_of(c * 256, 256), 256)]
+    firsts = []
+    for i, q in enumerate(far + near):
+        buf[0, q] = plain_dot(rows[q], out_rows).astype(BF)
+        firsts.append(sum_start(0, q, i))
+    seconds = [sum_over(0, m, firsts[m]) for m in range(2)]
+
+    down_rows = down_w[pl.ds(pl.multiple_of(c * 1024, 1024), 1024)]
+
+    def hidden_gradient(q):
+        grad_two[q] = (valid_all[q][:, :1] * cot_all[q].astype(F32)).astype(BF)
+        hgrad[q] = last_dot(grad_two[q], down_rows)
+
+    for m in range(2):
+        cots[2 + m].wait_recv()
+        hidden_gradient(near[m])
+    passed = []
+    for m in range(2):
+        cots[m].wait_recv()
+        got = cot_all.at[far[m], mine]
+        passed.append(send(got, got, c_s.at[4 + m], c_r.at[4 + m], core))
+    for m in range(2):
+        passed[m].wait_recv()
+        hidden_gradient(far[m])
+
+    spread = []
+    for m in range(2):
+        res = tok[m].astype(F32) + valid[m][:, :1] * sum_end(0, m, firsts[2 + m], seconds[m])
         resid[m] = res
         normed, _ = norm_rows(res)
-        own[m] = (normed * gain[1:2]).astype(BF)
-    column_spread(own, h_all, ss, rs, 6, b, y, c)
-
-
-def second_norm(part, tok, valid, gain):
-    return comm_call(
-        second_norm_body,
-        "second_norm",
-        4,
-        [((2, 96, 1024), F32), ((4, 2, 96, 1024), BF)],
-        SUM_SCRATCH + [pltpu.VMEM((2, 96, 1024), BF), dma(12), dma(12)],
-        4,
-    )(part, tok, valid, gain)
-
-
-def second_back_body(part, resid, cot, valid, gain, rgrad, ggrad, br_all, got, mid, fin, own, ss, rs):
-    b, y, z, x, c = place()
-    meet([(b + 1 - 2 * c, y), (b, 1 - y)])
-    sums = column_sum(part, got, mid, fin, ss, rs, b, y, c)
+        own[0, m] = (normed * gain[1:2]).astype(BF)
+        spread.append(spread_start(0, m, h_all))
+    done += firsts + seconds
+
+    def hidden_units(q):
+        pre = plain_dot(h_all[q], up_w[...])
+        phi = 0.5 * (1.0 + lax.erf(pre * ROOT_HALF))
+        hidden[q] = (pre * phi).astype(BF)
+        slope = phi + pre * DENSITY * jnp.exp(-0.5 * pre * pre)
+        pgrad[q] = (hgrad[q] * slope).astype(BF)
+        buf[1, q] = last_dot(pgrad[q], up_w[...]).astype(BF)
+
+    def second_branch(q, i):
+        buf[2, q] = plain_dot(hidden[q], down_rows).astype(BF)
+        return sum_start(2, q, i)
+
+    firsts, lasts = [None] * 4, [None] * 4
+    for m in range(2):
+        spread[m][1].wait_recv()
+        hidden_units(near[m])
+        firsts[2 + m] = sum_start(1, near[m], 2 + m)
+    passed2, seconds = [], []
+    for m in range(2):
+        passed2.append(spread_pass(0, m, h_all, spread[m]))
+        passed2[m].wait_recv()
+        hidden_units(far[m])
+        firsts[m] = sum_start(1, far[m], m)
+        lasts[2 + m] = second_branch(near[m], 2 + m)
+        seconds.append(sum_over(1, m, firsts[m]))
+
+    def weight_gradient(left, right, first_chunk):
+        for i in range(4):
+            block = left[:, :, i * 256 : i * 256 + 256].reshape(768, 256)
+            res = first_dot(block, right[...].reshape(768, 1024)).astype(BF)
+            for k in range(4):
+                part[first_chunk + k, i // 2, (i % 2) * 256 : (i % 2) * 256 + 256] = res[
+                    :, k * 256 : k * 256 + 256
+                ]
+
+    weight_gradient(hidden, grad_two, 0)
+
     total = jnp.zeros((1, 1024), F32)
-    for m in range(2):
+    bspread = []
+    for m in range(2):
+        e = sum_end(1, m, firsts[2 + m], seconds[m])
         normed, inv_std = norm_rows(resid[m])
-        e = sums[m]
         g = e * gain[1:2]
         total = total + jnp.sum(e * normed, axis=0, keepdims=True)
         one = jnp.mean(g, axis=-1, keepdims=True)
         two = jnp.mean(g * normed, axis=-1, keepdims=True)
         rg = cot[m].astype(F32) + (g - one - normed * two) * inv_std
         rgrad[m] = rg
-        own[m] = (valid[m][:, :1] * rg).astype(BF)
+        own[1, m] = (valid[m][:, :1] * rg).astype(BF)
+        bspread.append(spread_start(1, m, b_all))
     ggrad[...] = jnp.broadcast_to(total, (8, 1024))
-    column_spread(own, br_all, ss, rs, 6, b, y, c)
-
-
-def second_back(part, resid, cot, valid, gain):
+    done += firsts + seconds
+
+    for m in range(2):
+        lasts[m] = second_branch(far[m], m)
+    lseconds = [sum_over(2, m, lasts[m]) for m in range(2)]
+    weight_gradient(h_all, pgrad, 4)
+
+    def grad_copy(q, xd, i):
+        dest = q * 2 + xd
+        return dest, pltpu.make_async_remote_copy(
+            src_ref=agrad.at[q, :, pl.ds(xd * 128, 128)],
+            dst_ref=do.at[j],
+            send_sem=d_s.at[i, xd],
+            recv_sem=d_r.at[j],
+            device_id=(dest * 2 + c, y),
+            device_id_type=MESH,
+        )
+
+    def attention_gradient(q, i):
+        agrad[q] = last_dot(b_all[q], out_rows).astype(BF)
+        for xd in range(2):
+            dest, cp = grad_copy(q, xd, i)
+
+            @pl.when(dest != j)
+            def _():
+                cp.start()
+
+            @pl.when(dest == j)
+            def _():
+                do[j] = agrad[q, :, xd * 128 : xd * 128 + 128]
+
+    for m in range(2):
+        bspread[m][1].wait_recv()
+        attention_gradient(near[m], 2 + m)
+    passed3 = []
+    for m in range(2):
+        passed3.append(spread_pass(1, m, b_all, bspread[m]))
+        passed3[m].wait_recv()
+        attention_gradient(far[m], m)
+
+    res = first_dot(rows[...].reshape(768, 256), b_all[...].reshape(768, 1024)).astype(BF)
+    for h in range(2):
+        for k in range(2):
+            at = (h * 2 + k) * 256
+            part[8, h, k * 256 : k * 256 + 256] = res[:, at : at + 256]
+
+    for m in range(2):
+        branch = sum_end(2, m, lasts[2 + m], lseconds[m])
+        layer_out[m] = (resid[m] + valid[m][:, :1] * branch).astype(BF)
+    done += lasts + lseconds + cots + passed + passed2 + passed3
+    for pair in spread + bspread:
+        done += list(pair)
+    for cp in done:
+        cp.wait_send()
+    for i, q in enumerate(far + near):
+        for xd in range(2):
+            dest, cp = grad_copy(q, xd, i)
+
+            @pl.when(dest != j)
+            def _():
+                cp.wait_send()
+
+    for k in range(1, 8):
+        js = (j + k) % 8
+        pltpu.make_async_remote_copy(
+            src_ref=agrad.at[0, :, pl.ds(0, 128)],
+            dst_ref=do.at[js],
+            send_sem=d_s.at[0, 0],
+            recv_sem=d_r.at[js],
+            device_id=core,
+            device_id_type=MESH,
+        ).wait_recv()
+
+
+def middle(att, cot, tok, valid, valid_all, gain, out_w, up_w, down_w):
+    rows192 = (4, 192, 1024)
     return comm_call(
-        second_back_body,
-        "second_back",
-        5,
-        [((2, 96, 1024), F32), ((8, 1024), F32), ((4, 2, 96, 1024), BF)],
-        SUM_SCRATCH + [pltpu.VMEM((2, 96, 1024), BF), dma(12), dma(12)],
-        5,
-    )(part, resid, cot, valid, gain)
-
-
-def grad_heads_body(agrad, part, resid, valid, do, out, got, mid, fin, ss, rs):
-    b, y, z, x, c = place()
-    others = chips(b, c, y)
-    meet([(b + 1 - 2 * c, y), (b, 1 - y)] + [peer for _, peer in others])
-    j = b // 2
-    cps = []
-    for k, (jd, peer) in enumerate(others):
-        col = pl.multiple_of((jd % 2) * 128, 128)
-        cps.append(
-            send(agrad.at[jd // 2, :, pl.ds(col, 128)], do.at[j], ss.at[6 + k], rs.at[6 + k], peer)
-        )
-    do[j] = agrad[z, :, pl.ds(pl.multiple_of(x * 128, 128), 128)]
-    sums = column_sum(part, got, mid, fin, ss, rs, b, y, c)
-    for m in range(2):
-        out[m] = (resid[m] + valid[m][:, :1] * sums[m]).astype(BF)
-    for cp in cps:
-        cp.wait()
-
-
-def grad_heads(agrad, part, resid, valid):
-    return comm_call(
-        grad_heads_body,
-        "grad_heads",
-        6,
-        [((8, 192, 128), BF), ((2, 96, 1024), BF)],
-        SUM_SCRATCH + [dma(13), dma(13)],
-        4,
-    )(agrad, part, resid, valid)
+        middle_body,
+        "middle",
+        3,
+        [
+            ((8, 192, 128), BF),
+            ((2, 96, 1024), BF),
+            ((2, 96, 1024), F32),
+            ((8, 1024), F32),
+            ((9, 2, 512, 256), BF),
+        ],
+        [
+            pltpu.VMEM((4, 192, 256), BF),
+            pltpu.VMEM(rows192, BF),
+            pltpu.VMEM(rows192, BF),
+            pltpu.VMEM(rows192, BF),
+            pltpu.VMEM((3,) + rows192, BF),
+            pltpu.VMEM((3, 4, 96, 1024), BF),
+            pltpu.VMEM((3, 2, 96, 1024), BF),
+            pltpu.VMEM((3, 2, 96, 1024), BF),
+            pltpu.VMEM((2, 2, 96, 1024), BF),
+            pltpu.VMEM(rows192, BF),
+            pltpu.VMEM(rows192, F32),
+            pltpu.VMEM(rows192, BF),
+            pltpu.VMEM(rows192, BF),
+            pltpu.VMEM((4, 192, 256), BF),
+            pltpu.VMEM((2, 96, 1024), F32),
+            dma(7),
+            dma(7),
+            dma(6),
+            dma(6),
+            pltpu.SemaphoreType.DMA((3, 6)),
+            pltpu.SemaphoreType.DMA((3, 6)),
+            pltpu.SemaphoreType.DMA((2, 6)),
+            pltpu.SemaphoreType.DMA((2, 6)),
+            pltpu.SemaphoreType.DMA((4, 2)),
+            dma(8),
+        ],
+        9,
+    )(att, cot, tok, valid, valid_all, gain, out_w, up_w, down_w)
 
 
 def grad_rows_body(dqkv, rows, ss, rs):
@@ -1091,7 +1268,7 @@
     seg_row = jnp.broadcast_to(seg_z, (8, 1536))
     seg_col = jnp.broadcast_to(seg_z.reshape(1536, 1), (1536, 128))
     seg_here = lax.dynamic_slice_in_dim(seg_all, (z * 2 + x) * 192, 192, 1)
-    valid_all = (seg_here >= 0).astype(F32).reshape(768, 1)
+    valid_all = jnp.broadcast_to((seg_here >= 0).astype(F32)[:, :, None], (4, 192, 128))
     w_sel = w_sel.reshape(1024, 768)
     normed, _ = norm_rows(tok_all.reshape(768, 1024).astype(F32))
     h_one = (normed * gain[0:1]).astype(BF)
@@ -1100,52 +1277,24 @@
     up_sel = up_sel.reshape(1024, 1024)
     att = att.reshape(1536, 384)
     out_low, out_full, lse = attend(att, seg_col, seg_row)
-    attn_low, cot_all = from_heads(out_low.reshape(8, 192, 128), out_cotangent)
-    attn_low = attn_low.reshape(768, 256)
-    out_rows = lax.dynamic_slice_in_dim(out_weight, c * 256, 256, 0)
-    part = plain_dot(attn_low, out_rows).astype(BF)
-    resid, h_two = second_norm(part.reshape(4, 2, 96, 1024), tokens, valid, gain)
-    h_two = h_two.reshape(768, 1024)
-    pre_act = plain_dot(h_two, up_sel)
-    hidden_low = jax.nn.gelu(pre_act, approximate=False).astype(BF)
-    down_rows = lax.dynamic_slice_in_dim(down_weight, c * 1024, 1024, 0)
-    grad_two = (valid_all * cot_all.reshape(768, 1024).astype(F32)).astype(BF)
-    hidden_grad = last_dot(grad_two, down_rows)
-    slope = 0.5 * (1.0 + lax.erf(pre_act * ROOT_HALF)) + pre_act * DENSITY * jnp.exp(
-        -0.5 * pre_act * pre_act
-    )
-    pre_grad = (hidden_grad * slope).astype(BF)
-    e_part = last_dot(pre_grad, up_sel).astype(BF)
-    rgrad, gain_two_grad, branch = second_back(
-        e_part.reshape(4, 2, 96, 1024), resid, out_cotangent, valid, gain
-    )
-    branch = branch.reshape(768, 1024)
-    branch_two = plain_dot(hidden_low, down_rows).astype(BF)
-    first_dot = lambda a, d: lax.dot_general(
-        a, d, (((0,), (0,)), ((), ())), preferred_element_type=F32
-    )
-    down_grad = first_dot(hidden_low, grad_two)
-    up_grad = first_dot(h_two, pre_grad)
-    attn_grad = last_dot(branch, out_rows).astype(BF)
-    do, layer_out = grad_heads(
-        attn_grad.reshape(4, 192, 256), branch_two.reshape(4, 2, 96, 1024), resid, valid
-    )
-    outproj_grad = first_dot(attn_low, branch)
+    do, layer_out, rgrad, gain_two_grad, part = middle(
+        out_low.reshape(8, 192, 128),
+        out_cotangent,
+        tokens,
+        valid,
+        valid_all,
+        gain,
+        out_weight,
+        up_sel,
+        down_weight,
+    )
     dqkv = attend_back(att, out_full, lse, do.reshape(1536, 128), seg_col, seg_row)
     dqkv_rows = grad_rows(dqkv.reshape(8, 192, 384)).reshape(768, 768)
     c_part = last_dot(dqkv_rows, w_sel).astype(BF)
     token_grad, gain_one_grad = first_back(c_part.reshape(4, 2, 96, 1024), tokens, rgrad, gain)
     qkv_grad = first_dot(h_one, dqkv_rows)
     part = jnp.concatenate(
-        [
-            jnp.transpose(down_grad.astype(BF).reshape(2, 512, 4, 256), (2, 0, 1, 3)),
-            jnp.transpose(up_grad.astype(BF).reshape(2, 512, 4, 256), (2, 0, 1, 3)),
-            jnp.transpose(outproj_grad.astype(BF).reshape(256, 4, 256), (1, 0, 2)).reshape(
-                1, 2, 512, 256
-            ),
-            jnp.transpose(qkv_grad.astype(BF).reshape(2, 512, 3, 256), (2, 0, 1, 3)),
-        ],
-        0,
+        [part, jnp.transpose(qkv_grad.astype(BF).reshape(2, 512, 3, 256), (2, 0, 1, 3))], 0
     )
     rows8 = lax.broadcasted_iota(jnp.int32, (8, 1024), 0)
     full, gain_sum = weight_sums(part, jnp.where(rows8 == 0, gain_one_grad, gain_two_grad))

time: 510 us -> 438 us (0.86)
  matrix products: 43.8 us -> 8.9 us
  Pallas kernels: 424 us -> 402 us
  local copies, waits for them, and re-layouts: 26.7 us -> 13.4 us
    pallas_call x4 -> x1, Pallas kernels: 91.4 us -> 67.8 us  [middle(): comm_call(middle_body, 'middle', 3, [((8, 192, 128), BF), ((2, 96, 1024),...]
    dot_general x4 -> x1, matrix products: 18.1 us -> 2.41 us  [plain_dot(): lax.dot_general(a, b, (((1,), (0,)), ((), ())), preferred_element_type=F32)]
    dot_general x4 -> x1, matrix products: 14.4 us -> 3.94 us  [first_dot(): lax.dot_general(a, d, (((0,), (0,)), ((), ())), preferred_element_type=F32)]
    dot_general x4 -> x1, matrix products: 11.3 us -> 2.56 us  [last_dot(): lax.dot_general(a, b, (((1,), (1,)), ((), ())), preferred_element_type=F32)]
    reshape x3 -> x0, local copies, waits for them, and re-layouts: 7.85 us -> none  [the longest x1 4.49 us: column_device(): down_grad.astype(BF).reshape(2, 512, 4, 256)]
where the time goes in v3:
time: 438 us; the launch traced here: 437 us
  Pallas kernels  402 us (92%)
  local copies, waits for them, and re-layouts  13.4 us (3%)
  other arithmetic  11.3 us (3%)
  matrix products  8.9 us (2%)
    pallas_call x1, Pallas kernels, weight_sums(): pl.pallas_call(wsum_body, out_shape=[jax.ShapeDtypeStruct((CHUNKS, 2, 2,...  179 us
    pallas_call x1, Pallas kernels, middle(): comm_call(middle_body, 'middle', 3, [((8, 192, 128), BF), ((2, 96, 1024),...  67.8 us
    pallas_call x1, Pallas kernels, open_call(): comm_call(open_body, 'open_column', 1, [((4, 2, 96, 1024), BF), ((2, 2, 1...  34.2 us
    pallas_call x1, Pallas kernels, to_heads(): comm_call(to_heads_body, 'to_heads', 2, [((8, 192, 384), BF), ((2, 512, 1...  32 us
    pallas_call x1, Pallas kernels, grad_rows(): comm_call(grad_rows_body, 'grad_rows', 7, [((4, 192, 768), BF)], [dma(7),...  25.9 us
    pallas_call x1, Pallas kernels, attend_back(): pl.pallas_call(attend_back_body, grid=(length // rows,), in_specs=[wide,...  17.1 us
    pallas_call x1, Pallas kernels, first_back(): comm_call(first_back_body, 'first_back', 8, [((2, 96, 1024), F32), ((8, 1...  14.8 us
    pallas_call x1, Pallas kernels, attend(): pl.pallas_call(attend_body, grid=(length // rows,), in_specs=[pl.BlockSpe...  12.4 us

profile of v3, /device:TPU:0, one launch (start us, length us, event | category | flops | bytes accessed | tf_op | source)
XLA Modules:
  0.0 436.9 jit_solution(16543777684274480050)
XLA Ops:
  0.7 0.8 compare_convert_fusion
  1.4 0.7 stack.9
  2.1 0.7 stack.10
  2.8 0.6 fusion.8.gains
  3.4 0.7 broadcast_in_dim.13.valid
  4.2 34.2 %open_column.1 = (bf16[4,2,96,1024]{3,2,1,0:T(8,128)(2,1)}, s32[2,2,1536]{2,1,0:T(2,128)}, bf16[2,512,768]{2,1,0:T(8,128)(2,1)}, f32[2,8,512]{2,1,0:T(8,128)}) custom-call(bf16[2,96,1024]{2,1,0:T(8,128)(2,1)} %tok.5, s32[2,1536]{1,0:T(2,128)} %seg.1, bf16[512,3072]{1,0:T(8,128)(2,1)} %wqkv.1, f32[8,512]{1,0:T(8,128)} %fusion.8.gains), custom_call_target="tpu_custom_call" | custom-call | tf_op jit(solution)/shard_map/open_column/pallas_call | solution.py:426
  38.3 0.9 slice.13
  39.2 1.7 convert_reduce_fusion
  40.9 0.6 fusion.2
  42.4 0.6 broadcast_in_dim.12.seg_row
  43.0 0.9 broadcast_in_dim.14.valid_all
  44.0 1.1 broadcast_in_dim.11.seg_col
  45.1 2.4 convolution_convert_fusion.2
  47.5 32.0 %to_heads.1 = (bf16[8,192,384]{2,1,0:T(8,128)(2,1)}, bf16[2,512,1024]{2,1,0:T(8,128)(2,1)}) custom-call(bf16[4,192,768]{2,1,0:T(8,128)(2,1)} %bitcast.35, bf16[512,4096]{1,0:T(8,128)(2,1)} %up.1), custom_call_target="tpu_custom_call" | custom-call | tf_op jit(solution)/shard_map/to_heads/pallas_call | solution.py:467
  79.6 12.4 %attend.1 = (bf16[1536,128]{1,0:T(8,128)(2,1)}, f32[1536,128]{1,0:T(8,128)}, f32[1536,128]{1,0:T(8,128)}) custom-call(bf16[1536,384]{1,0:T(8,128)(2,1)} %bitcast.26, s32[1536,128]{1,0:T(8,128)} %broadcast_in_dim.11.seg_col, s32[8,1536]{1,0:T(8,128)} %broadcast_in_dim.12.seg_row), custom_call_target="tpu_custom_call" | custom-call | tf_op jit(solution)/shard_map/attend/pallas_call | solution.py:914
  91.9 67.8 %middle.1 = (bf16[8,192,128]{2,1,0:T(8,128)(2,1)}, bf16[2,96,1024]{2,1,0:T(8,128)(2,1)}, f32[2,96,1024]{2,1,0:T(8,128)}, f32[8,1024]{1,0:T(8,128)}, bf16[9,2,512,256]{3,2,1,0:T(8,128)(2,1)}) custom-call(bf16[8,192,128]{2,1,0:T(8,128)(2,1)} %bitcast.36, bf16[2,96,1024]{2,1,0:T(8,128)(2,1)} %cot.1, bf16[2,96,1024]{2,1,0:T(8,128)(2,1)} %tok.5, ...), custom_call_target="tpu_custom_call" | custom-call | tf_op jit(solution)/shard_map/middle/pallas_call | solution.py:790
  159.8 17.1 %attend_back.1 = bf16[1536,384]{1,0:T(8,128)(2,1)} custom-call(bf16[1536,384]{1,0:T(8,128)(2,1)} %bitcast.27, f32[1536,128]{1,0:T(8,128)} %get-tuple-element.34.out, f32[1536,128]{1,0:T(8,128)} %get-tuple-element.35.lse, bf16[1536,128]{1,0:T(8,128)(2,1)} %bitcast.37, s32[1536,128]{1,0:T(8,128)} %broadcast_in_dim.11.seg_col, s32[8,1536]{1,0:T(8,128)} %broadcast_in_dim.12.seg_row), custom_call_target="tpu_custom_call" | custom-call | tf_op jit(solution)/shard_map/attend_back/pallas_call | solution.py:980
  176.9 25.9 %grad_rows.1 = bf16[4,192,768]{2,1,0:T(8,128)(2,1)} custom-call(bf16[8,192,384]{2,1,0:T(8,128)(2,1)} %bitcast.28), custom_call_target="tpu_custom_call" | custom-call | tf_op jit(solution)/shard_map/grad_rows/pallas_call | solution.py:846
  202.8 3.9 convolution_convert_fusion
  206.8 2.6 convolution_convert_fusion.1
  209.3 14.8 %first_back.1 = (f32[2,96,1024]{2,1,0:T(8,128)}, f32[8,1024]{1,0:T(8,128)}) custom-call(bf16[4,2,96,1024]{3,2,1,0:T(8,128)(2,1)} %bitcast.32, bf16[2,96,1024]{2,1,0:T(8,128)(2,1)} %tok.5, f32[2,96,1024]{2,1,0:T(8,128)} %get-tuple-element.37.rgrad, f32[8,1024]{1,0:T(8,128)} %bitcast.40), custom_call_target="tpu_custom_call" | custom-call | tf_op jit(solution)/shard_map/first_back/pallas_call | solution.py:868
  224.1 1.4 broadcast_select_fusion.gg
  225.6 4.2 reshape.126
  230.0 5.6 %pad_maximum_fusion.part = bf16[12,2,512,256]{3,2,1,0:T(8,128)(2,1)} fusion(bf16[3,2,512,256]{3,2,1,0:T(8,128)(2,1)S(1)} %bitcast.25, bf16[9,2,512,256]{3,2,1,0:T(8,128)(2,1)} %get-tuple-element.39), kind=kLoop, calls=%fused_computation | loop fusion | flops 3145728 | bytes 12582912 | tf_op jit(solution)/shard_map/concatenate | solution.py:1296
  235.6 178.5 %weight_sums.1 = (bf16[12,2,2,512,256]{4,3,2,1,0:T(8,128)(2,1)}, f32[8,1024]{1,0:T(8,128)}) custom-call(bf16[12,2,512,256]{3,2,1,0:T(8,128)(2,1)} %pad_maximum_fusion.part, f32[8,1024]{1,0:T(8,128)} %broadcast_select_fusion.gg), custom_call_target="tpu_custom_call" | custom-call | tf_op jit(solution)/shard_map/weight_sums/pallas_call | solution.py:1163
  414.1 1.5 fusion.10
  415.6 2.4 widen_out.1
  418.0 5.2 %widen_qkv.1 = f32[512,3072]{1,0:T(8,128)} custom-call(bf16[12,2,2,512,256]{4,3,2,1,0:T(8,128)(2,1)} %get-tuple-element.42.src), custom_call_target="tpu_custom_call" | custom-call | tf_op jit(solution)/shard_map/widen_qkv/pallas_call | solution.py:1238
  423.2 6.0 %widen_down.1 = f32[2048,1024]{1,0:T(8,128)} custom-call(bf16[12,2,2,512,256]{4,3,2,1,0:T(8,128)(2,1)} %get-tuple-element.42.src), custom_call_target="tpu_custom_call" | custom-call | tf_op jit(solution)/shard_map/widen_down/pallas_call | solution.py:1214
  429.2 6.1 %widen_up.1 = f32[512,4096]{1,0:T(8,128)} custom-call(bf16[12,2,2,512,256]{4,3,2,1,0:T(8,128)(2,1)} %get-tuple-element.42.src), custom_call_target="tpu_custom_call" | custom-call | tf_op jit(solution)/shard_map/widen_up/pallas_call | solution.py:1222
  435.3 0.7 copy.25
  436.0 0.9 copy.26
  (22 shorter events, 1.1 us)
Async XLA Ops:
  38.3 2.6 copy-start
  41.5 0.7 copy-start.5
  41.5 3.6 copy-start.6
  202.8 4.0 copy-start.1
  209.3 14.8 %copy-start.4 = (f32[8,1024]{1,0:T(8,128)S(1)}, f32[8,1024]{1,0:T(8,128)}, u32[]{:S(2)}) copy-start(f32[8,1024]{1,0:T(8,128)} %get-tuple-element.41) | copy-start | bytes 98308
  429.2 6.1 %copy-start.3 = (bf16[2,96,1024]{2,1,0:T(8,128)(2,1)S(1)}, bf16[2,96,1024]{2,1,0:T(8,128)(2,1)}, u32[]{:S(2)}) copy-start(bf16[2,96,1024]{2,1,0:T(8,128)(2,1)} %get-tuple-element.54) | copy-start | bytes 1179652
  429.2 6.8 %copy-start.2 = (f32[2,96,1024]{2,1,0:T(8,128)S(1)}, f32[2,96,1024]{2,1,0:T(8,128)}, u32[]{:S(2)}) copy-start(f32[2,96,1024]{2,1,0:T(8,128)} %get-tuple-element.55) | copy-start | bytes 2359300

commit v4 on v3

--- a/solution.py
+++ b/solution.py
@@ -472,59 +472,6 @@
         [dma(8), dma(8)],
         2,
     )(qkv, up)
-
-
-def column_sum(part, got, mid, fin, ss, rs, b, y, c):
-    core, over = (b + 1 - 2 * c, y), (b, 1 - y)
-    first = []
-    for m in range(2):
-        q = 2 * (1 - y) + m
-        first.append(send(part.at[q, 1 - c], got.at[q], ss.at[m], rs.at[m], core))
-    for m in range(2):
-        q = 2 * y + m
-        first.append(send(part.at[q, 1 - c], got.at[q], ss.at[2 + m], rs.at[2 + m], core))
-    second = []
-    for m in range(2):
-        q = 2 * (1 - y) + m
-        first[m].wait_recv()
-        mid[m] = (part[q, c].astype(F32) + got[q].astype(F32)).astype(BF)
-        second.append(send(mid.at[m], fin.at[m], ss.at[4 + m], rs.at[4 + m], over))
-    sums = []
-    for m in range(2):
-        q = 2 * y + m
-        first[2 + m].wait_recv()
-        second[m].wait_recv()
-        sums.append(part[q, c].astype(F32) + got[q].astype(F32) + fin[m].astype(F32))
-    for cp in first + second:
-        cp.wait_send()
-    return sums
-
-
-def column_spread(own, full, ss, rs, k, b, y, c):
-    core, over = (b + 1 - 2 * c, y), (b, 1 - y)
-    near, side = [], []
-    for m in range(2):
-        near.append(send(own.at[m], full.at[2 * y + m, c], ss.at[k], rs.at[k], over))
-        side.append(send(own.at[m], full.at[2 * y + m, c], ss.at[k + 1], rs.at[k + 1], core))
-        k += 2
-    for m in range(2):
-        full[2 * y + m, c] = own[m]
-    for m in range(2):
-        near[m].wait_recv()
-        got = full.at[2 * (1 - y) + m, c]
-        side.append(send(got, got, ss.at[k], rs.at[k], core))
-        k += 1
-    for cp in near:
-        cp.wait_send()
-    for cp in side:
-        cp.wait()
-
-
-SUM_SCRATCH = [
-    pltpu.VMEM((4, 96, 1024), BF),
-    pltpu.VMEM((2, 96, 1024), BF),
-    pltpu.VMEM((2, 96, 1024), BF),
-]
 
 
 def first_dot(a, d):
@@ -829,52 +776,6 @@
     )(att, cot, tok, valid, valid_all, gain, out_w, up_w, down_w)
 
 
-def grad_rows_body(dqkv, rows, ss, rs):
-    b, y, z, x, c = place()
-    others = chips(b, c, y)
-    meet([peer for _, peer in others])
-    col = pl.multiple_of(x * 384, 128)
-    cps = []
-    for k, (jd, peer) in enumerate(others):
-        cps.append(send(dqkv.at[jd], rows.at[z, :, pl.ds(col, 384)], ss.at[k], rs.at[k], peer))
-    rows[z, :, pl.ds(col, 384)] = dqkv[b // 2]
-    for cp in cps:
-        cp.wait()
-
-
-def grad_rows(dqkv):
-    return comm_call(
-        grad_rows_body, "grad_rows", 7, [((4, 192, 768), BF)], [dma(7), dma(7)], 1
-    )(dqkv)[0]
-
-
-def first_back_body(part, tok, rgrad, gain, tgrad, ggrad, got, mid, fin, ss, rs):
-    b, y, z, x, c = place()
-    meet([(b + 1 - 2 * c, y), (b, 1 - y)])
-    sums = column_sum(part, got, mid, fin, ss, rs, b, y, c)
-    total = jnp.zeros((1, 1024), F32)
-    for m in range(2):
-        normed, inv_std = norm_rows(tok[m].astype(F32))
-        e = sums[m]
-        g = e * gain[0:1]
-        total = total + jnp.sum(e * normed, axis=0, keepdims=True)
-        one = jnp.mean(g, axis=-1, keepdims=True)
-        two = jnp.mean(g * normed, axis=-1, keepdims=True)
-        tgrad[m] = rgrad[m] + (g - one - normed * two) * inv_std
-    ggrad[...] = jnp.broadcast_to(total, (8, 1024))
-
-
-def first_back(part, tok, rgrad, gain):
-    return comm_call(
-        first_back_body,
-        "first_back",
-        8,
-        [((2, 96, 1024), F32), ((8, 1024), F32)],
-        SUM_SCRATCH + [dma(6), dma(6)],
-        4,
-    )(part, tok, rgrad, gain)
-
-
 def last_dot(a, b):
     return lax.dot_general(a, b, (((1,), (1,)), ((), ())), preferred_element_type=F32)
 
@@ -1002,11 +903,12 @@
 
 CHUNKS = 12
 SWAPPED = ((4, 8), (9, 12))
-
-
-def wsum_body(part, gg, full, gsum, r1, s1, r2, s2, r3, p3, tmp, g1, g2, g3, ss, rs, ls, gs, gr):
+PLAIN = ((0, 4), (8, 9))
+STAGES = 5
+
+
+def chunk_sums(part, full, r1, r2, r3, p3, tmp, ss, rs, ls):
     b, y, z, x, c = place()
-    others = chips(b, c, y)
     z0, zb = z % 2, z // 2
     core, over = (b + 1 - 2 * c, y), (b, 1 - y)
     px, p0, pb = (b + 2 - 4 * x, y), (b + 4 - 8 * z0, y), (b + 8 - 16 * zb, y)
@@ -1014,8 +916,8 @@
     o2 = o1 + z0 * 128
     o3 = o2 + zb * 64
 
-    def rows(start, size):
-        return pl.ds(pl.multiple_of(start, 64), size)
+    def rows(at, size):
+        return pl.ds(pl.multiple_of(at, 64), size)
 
     def remote(src, dst, stage, i, peer):
         return pltpu.make_async_remote_copy(
@@ -1031,10 +933,10 @@
         return remote(part.at[i, :, rows((1 - x) * 256, 256)], r1.at[i], 0, i, px)
 
     def c_z0(i):
-        return remote(s1.at[i, :, rows((1 - z0) * 128, 128)], r2.at[i], 1, i, p0)
+        return remote(part.at[i, :, rows(o1 + (1 - z0) * 128, 128)], r2.at[i], 1, i, p0)
 
     def c_zb(i):
-        return remote(s2.at[i, :, rows((1 - zb) * 64, 64)], r3.at[i], 2, i, pb)
+        return remote(part.at[i, :, rows(o2 + (1 - zb) * 64, 64)], r3.at[i], 2, i, pb)
 
     def c_y(i):
         return remote(tmp.at[i], p3.at[i, y], 3, i, over)
@@ -1057,44 +959,21 @@
         src = full.at[i, c]
         return remote(src, src, 7, i, core)
 
-    meet([core, over] + [peer for _, peer in others])
-
-    @pl.loop(0, CHUNKS)
-    def _(i):
-        c_x(i).start()
-
-    gcps = [send(gg, g1.at[0], gs.at[0], gr.at[0], core)]
-    gcps[0].wait_recv()
-    g1[1] = g1[0] + gg[...]
-    gcps.append(send(g1.at[1], g2.at[0], gs.at[1], gr.at[1], over))
-    gcps[1].wait_recv()
-    j = b // 2
-    g3[j] = g1[1] + g2[0]
-    for k, (jd, peer) in enumerate(others):
-        gcps.append(send(g3.at[j], g3.at[j], gs.at[2 + k], gr.at[2 + k], peer))
-
-    def when_chunk(t, lag, act, ranges=((0, CHUNKS),)):
-        for lo, hi in ranges:
-
-            @pl.when((t - lag >= lo) & (t - lag < hi))
-            def _():
-                act(t - lag)
-
     def add_x(i):
         c_x(i).wait_recv()
-        mine = part[i, :, rows(x * 256, 256)].astype(F32)
-        s1[i] = (mine + r1[i].astype(F32)).astype(BF)
+        mine = part[i, :, rows(o1, 256)].astype(F32)
+        part[i, :, rows(o1, 256)] = (mine + r1[i].astype(F32)).astype(BF)
         c_z0(i).start()
 
     def add_z0(i):
         c_z0(i).wait_recv()
-        mine = s1[i, :, rows(z0 * 128, 128)].astype(F32)
-        s2[i] = (mine + r2[i].astype(F32)).astype(BF)
+        mine = part[i, :, rows(o2, 128)].astype(F32)
+        part[i, :, rows(o2, 128)] = (mine + r2[i].astype(F32)).astype(BF)
         c_zb(i).start()
 
     def add_zb_plain(i):
         c_zb(i).wait_recv()
-        mine = s2[i, :, rows(zb * 64, 64)].astype(F32)
+        mine = part[i, :, rows(o3, 64)].astype(F32)
         p3[i] = (mine + r3[i].astype(F32)).astype(BF)
         c_gb(i).start()
         c_own(i).start()
@@ -1102,7 +981,7 @@
     def add_zb_swap(i):
         c_zb(i).wait_recv()
         for h, dst in ((y, p3.at[i, y]), (1 - y, tmp.at[i])):
-            mine = s2[i, h, rows(zb * 64, 64)].astype(F32)
+            mine = part[i, h, rows(o3, 64)].astype(F32)
             dst[...] = (mine + r3[i, h].astype(F32)).astype(BF)
         c_y(i).start()
 
@@ -1120,74 +999,219 @@
         c_g0(i).wait_recv()
         c_gx(i).start()
 
-    def grow_core(i):
-        c_gx(i).wait_recv()
-        c_core(i).start()
-
-    plain = ((0, 4), (8, 9))
-
-    @pl.loop(0, CHUNKS + 6)
+    def when_chunk(i, act, ranges=((0, CHUNKS),)):
+        for lo, hi in ranges:
+            if isinstance(i, int):
+                if lo <= i < hi:
+                    act(i)
+                continue
+
+            @pl.when((i >= lo) & (i < hi))
+            def _():
+                act(i)
+
+    def tick(t):
+        when_chunk(t - 5, grow_x)
+        when_chunk(t - 4, grow_z0)
+        when_chunk(t - 3, take_y, SWAPPED)
+        when_chunk(t - 2, add_zb_plain, PLAIN)
+        when_chunk(t - 2, add_zb_swap, SWAPPED)
+        when_chunk(t - 1, add_z0)
+        when_chunk(t, add_x)
+
+    def finish():
+        @pl.loop(0, CHUNKS)
+        def _(i):
+            c_gx(i).wait_recv()
+            c_core(i).start()
+
+        @pl.loop(0, CHUNKS)
+        def _(i):
+            c_core(i).wait_recv()
+            for cp in (c_x, c_z0, c_zb, c_gb, c_g0, c_gx, c_core):
+                cp(i).wait_send()
+
+        for lo, hi in SWAPPED:
+
+            @pl.loop(lo, hi)
+            def _(i):
+                c_y(i).wait_send()
+
+    def start(i):
+        c_x(i).start()
+
+    return start, tick, finish
+
+
+def chunk_scratch():
+    return [
+        pltpu.VMEM((CHUNKS, 2, 512, 256), BF),
+        pltpu.VMEM((CHUNKS, 2, 256, 256), BF),
+        pltpu.VMEM((CHUNKS, 2, 128, 256), BF),
+        pltpu.VMEM((CHUNKS, 2, 64, 256), BF),
+        pltpu.VMEM((CHUNKS, 2, 64, 256), BF),
+        pltpu.VMEM((CHUNKS, 64, 256), BF),
+        pltpu.SemaphoreType.DMA((8, CHUNKS)),
+        pltpu.SemaphoreType.DMA((8, CHUNKS)),
+        pltpu.SemaphoreType.DMA((CHUNKS,)),
+    ]
+
+
+def tail_body(
+    dqkv,
+    parts,
+    w_sel,
+    h_one,
+    tok,
+    rgrad,
+    gain,
+    gg,
+    tgrad,
+    full,
+    gsum,
+    rows,
+    buf,
+    gots,
+    mids,
+    fins,
+    g1,
+    g2,
+    g3,
+    a_s,
+    a_r,
+    r_s,
+    r_r,
+    g_s,
+    g_r,
+    l_s,
+    part,
+    r1,
+    r2,
+    r3,
+    p3,
+    tmp,
+    ss,
+    rs,
+    ls,
+):
+    b, y, z, x, c = place()
+    core, over = (b + 1 - 2 * c, y), (b, 1 - y)
+    j = b // 2
+    others = chips(b, c, y)
+    mine = pl.ds(pl.multiple_of(c * 96, 32), 96)
+    theirs = pl.ds(pl.multiple_of((1 - c) * 96, 32), 96)
+    far = [2 * (1 - y) + m for m in range(2)]
+    near = [2 * y + m for m in range(2)]
+    start, tick, finish = chunk_sums(part, full, r1, r2, r3, p3, tmp, ss, rs, ls)
+    load = pltpu.make_async_copy(parts, part.at[0:9], l_s.at[0])
+    load.start()
+    meet([core, over] + [peer for _, peer in others])
+    col = pl.multiple_of(x * 384, 128)
+    done = []
+    for k, (jd, peer) in enumerate(others):
+        done.append(send(dqkv.at[jd], rows.at[z, :, pl.ds(col, 384)], a_s.at[k], a_r.at[k], peer))
+    rows[z, :, pl.ds(col, 384)] = dqkv[j]
+    load.wait()
+    for i in range(9):
+        start(i)
+    for t in range(2):
+        tick(t)
+    for cp in done:
+        cp.wait_recv()
+    firsts = []
+    for i, q in enumerate(far + near):
+        buf[q] = last_dot(rows[q], w_sel[...]).astype(BF)
+        firsts.append(
+            send(buf.at[q, theirs], gots.at[q], r_s.at[i], r_r.at[i], core)
+        )
+    seconds = []
+    for m in range(2):
+        firsts[m].wait_recv()
+        q = far[m]
+        mids[m] = (buf[q, mine].astype(F32) + gots[q].astype(F32)).astype(BF)
+        seconds.append(send(mids.at[m], fins.at[m], r_s.at[4 + m], r_r.at[4 + m], over))
+    for i in range(4):
+        block = h_one[:, :, i * 256 : i * 256 + 256].reshape(768, 256)
+        res = first_dot(block, rows[...].reshape(768, 768)).astype(BF)
+        for k in range(3):
+            part[9 + k, i // 2, (i % 2) * 256 : (i % 2) * 256 + 256] = res[
+                :, k * 256 : k * 256 + 256
+            ]
+    for i in range(9, 12):
+        start(i)
+    total = jnp.zeros((1, 1024), F32)
+    for m in range(2):
+        tick(2 + m)
+        firsts[2 + m].wait_recv()
+        seconds[m].wait_recv()
+        q = near[m]
+        e = buf[q, mine].astype(F32) + gots[q].astype(F32) + fins[m].astype(F32)
+        normed, inv_std = norm_rows(tok[m].astype(F32))
+        g = e * gain[0:1]
+        total = total + jnp.sum(e * normed, axis=0, keepdims=True)
+        one = jnp.mean(g, axis=-1, keepdims=True)
+        two = jnp.mean(g * normed, axis=-1, keepdims=True)
+        tgrad[m] = rgrad[m] + (g - one - normed * two) * inv_std
+    g1[1] = jnp.where(lax.broadcasted_iota(jnp.int32, (8, 1024), 0) == 0, total, gg[...])
+    gcps = [send(g1.at[1], g1.at[0], g_s.at[0], g_r.at[0], core)]
+    tick(4)
+    gcps[0].wait_recv()
+    g2[1] = g1[0] + g1[1]
+    gcps.append(send(g2.at[1], g2.at[0], g_s.at[1], g_r.at[1], over))
+    tick(5)
+    gcps[1].wait_recv()
+    g3[j] = g2[1] + g2[0]
+    for k, (jd, peer) in enumerate(others):
+        gcps.append(send(g3.at[j], g3.at[j], g_s.at[2 + k], g_r.at[2 + k], peer))
+
+    @pl.loop(6, CHUNKS + STAGES)
     def _(t):
-        when_chunk(t, 6, grow_core)
-        when_chunk(t, 5, grow_x)
-        when_chunk(t, 4, grow_z0)
-        when_chunk(t, 3, take_y, SWAPPED)
-        when_chunk(t, 2, add_zb_plain, plain)
-        when_chunk(t, 2, add_zb_swap, SWAPPED)
-        when_chunk(t, 1, add_z0)
-        when_chunk(t, 0, add_x)
-
-    @pl.loop(0, CHUNKS)
-    def _(i):
-        c_core(i).wait_recv()
-        for cp in (c_x, c_z0, c_zb, c_gb, c_g0, c_gx, c_core):
-            cp(i).wait_send()
-
-    for lo, hi in SWAPPED:
-
-        @pl.loop(lo, hi)
-        def _(i):
-            c_y(i).wait_send()
-
-    for cp in gcps[:2]:
+        tick(t)
+
+    finish()
+    for cp in gcps[:2] + done + firsts + seconds:
         cp.wait_send()
     for cp in gcps[2:]:
         cp.wait()
-    total = g3[0]
+    res = g3[0]
     for k in range(1, 8):
-        total = total + g3[k]
-    gsum[...] = total
-
-
-def weight_sums(part, gg):
+        res = res + g3[k]
+    gsum[...] = res
+
+
+def tail(dqkv, parts, w_sel, h_one, tok, rgrad, gain, gg):
+    vm = pl.BlockSpec(memory_space=pltpu.VMEM)
+    hbm = pl.BlockSpec(memory_space=pl.ANY)
     return pl.pallas_call(
-        wsum_body,
+        tail_body,
         out_shape=[
+            jax.ShapeDtypeStruct((2, 96, 1024), F32),
             jax.ShapeDtypeStruct((CHUNKS, 2, 2, 512, 256), BF),
             jax.ShapeDtypeStruct((8, 1024), F32),
         ],
-        in_specs=[pl.BlockSpec(memory_space=pltpu.VMEM)] * 2,
-        out_specs=[pl.BlockSpec(memory_space=pl.ANY), pl.BlockSpec(memory_space=pltpu.VMEM)],
+        in_specs=[vm, hbm] + [vm] * 6,
+        out_specs=[vm, hbm, vm],
         scratch_shapes=[
-            pltpu.VMEM((CHUNKS, 2, 256, 256), BF),
-            pltpu.VMEM((CHUNKS, 2, 256, 256), BF),
-            pltpu.VMEM((CHUNKS, 2, 128, 256), BF),
-            pltpu.VMEM((CHUNKS, 2, 128, 256), BF),
-            pltpu.VMEM((CHUNKS, 2, 64, 256), BF),
-            pltpu.VMEM((CHUNKS, 2, 64, 256), BF),
-            pltpu.VMEM((CHUNKS, 64, 256), BF),
+            pltpu.VMEM((4, 192, 768), BF),
+            pltpu.VMEM((4, 192, 1024), BF),
+            pltpu.VMEM((4, 96, 1024), BF),
+            pltpu.VMEM((2, 96, 1024), BF),
+            pltpu.VMEM((2, 96, 1024), BF),
             pltpu.VMEM((2, 8, 1024), F32),
-            pltpu.VMEM((1, 8, 1024), F32),
+            pltpu.VMEM((2, 8, 1024), F32),
             pltpu.VMEM((8, 8, 1024), F32),
-            pltpu.SemaphoreType.DMA((8, CHUNKS)),
-            pltpu.SemaphoreType.DMA((8, CHUNKS)),
-            pltpu.SemaphoreType.DMA((CHUNKS,)),
+            dma(7),
+            dma(7),
+            dma(6),
+            dma(6),
             dma(9),
             dma(9),
-        ],
-        compiler_params=pltpu.CompilerParams(collective_id=9, has_side_effects=True),
-        name="weight_sums",
-    )(part, gg)
+            dma(1),
+        ]
+        + chunk_scratch(),
+        compiler_params=pltpu.CompilerParams(collective_id=4, has_side_effects=True),
+        name="tail",
+    )(dqkv, parts, w_sel, h_one, tok, rgrad, gain, gg)
 
 
 def widen_body(src, dst):
@@ -1289,15 +1313,16 @@
         down_weight,
     )
     dqkv = attend_back(att, out_full, lse, do.reshape(1536, 128), seg_col, seg_row)
-    dqkv_rows = grad_rows(dqkv.reshape(8, 192, 384)).reshape(768, 768)
-    c_part = last_dot(dqkv_rows, w_sel).astype(BF)
-    token_grad, gain_one_grad = first_back(c_part.reshape(4, 2, 96, 1024), tokens, rgrad, gain)
-    qkv_grad = first_dot(h_one, dqkv_rows)
-    part = jnp.concatenate(
-        [part, jnp.transpose(qkv_grad.astype(BF).reshape(2, 512, 3, 256), (2, 0, 1, 3))], 0
-    )
-    rows8 = lax.broadcasted_iota(jnp.int32, (8, 1024), 0)
-    full, gain_sum = weight_sums(part, jnp.where(rows8 == 0, gain_one_grad, gain_two_grad))
+    token_grad, full, gain_sum = tail(
+        dqkv.reshape(8, 192, 384),
+        part,
+        w_sel,
+        h_one.reshape(4, 192, 1024),
+        tokens,
+        rgrad,
+        gain,
+        gain_two_grad,
+    )
     down_out, up_out, out_out, qkv_out = widen_all(full)
     gain_out = lax.dynamic_slice_in_dim(gain_sum, y * 512, 512, 1)
     return (

time: 438 us -> 367 us (0.84)
  Pallas kernels: 402 us -> 347 us
  matrix products: 8.9 us -> 2.41 us
  local copies, waits for them, and re-layouts: 13.4 us -> 8.98 us
    pallas_call x3 -> x1, Pallas kernels: 219 us -> 163 us  [tail(): pl.pallas_call(tail_body, out_shape=[jax.ShapeDtypeStruct((2, 96, 1024),...]
    dot_general x2 -> x0, matrix products: 6.5 us -> none  [the longest x1 3.94 us: first_dot(): lax.dot_general(a, d, (((0,), (0,)), ((), ())), preferred_element_type=F32)]
    concatenate x1 -> x0, other arithmetic: 5.58 us -> none  [column_device(): jnp.concatenate([part, jnp.transpose(qkv_grad.astype(BF).reshape(2, 512,...]
where the time goes in v4:
time: 367 us; the launch traced here: 366 us
  Pallas kernels  347 us (95%)
  local copies, waits for them, and re-layouts  8.98 us (2%)
  other arithmetic  7.36 us (2%)
    pallas_call x1, Pallas kernels, tail(): pl.pallas_call(tail_body, out_shape=[jax.ShapeDtypeStruct((2, 96, 1024),...  163 us
    pallas_call x1, Pallas kernels, middle(): comm_call(middle_body, 'middle', 3, [((8, 192, 128), BF), ((2, 96, 1024),...  67.9 us
    pallas_call x1, Pallas kernels, open_call(): comm_call(open_body, 'open_column', 1, [((4, 2, 96, 1024), BF), ((2, 2, 1...  34.3 us
    pallas_call x1, Pallas kernels, to_heads(): comm_call(to_heads_body, 'to_heads', 2, [((8, 192, 384), BF), ((2, 512, 1...  32 us
    pallas_call x1, Pallas kernels, attend_back(): pl.pallas_call(attend_back_body, grid=(length // rows,), in_specs=[wide,...  17.1 us
    pallas_call x1, Pallas kernels, attend(): pl.pallas_call(attend_body, grid=(length // rows,), in_specs=[pl.BlockSpe...  12.4 us
    pallas_call x2, Pallas kernels, widen_all(): pl.pallas_call(widen_body, grid=(4,), in_specs=[pl.BlockSpec((4, None, No...  12 us

profile of v4, /device:TPU:0, one launch (start us, length us, event | category | flops | bytes accessed | tf_op | source)
XLA Modules:
  0.0 366.2 jit_solution(12131210526701065460)
XLA Ops:
  0.7 0.8 compare_convert_fusion
  1.4 0.7 stack.9
  2.1 0.7 stack.10
  2.8 0.6 fusion.6.gains
  3.4 0.7 broadcast_in_dim.13.valid
  4.2 34.3 %open_column.1 = (bf16[4,2,96,1024]{3,2,1,0:T(8,128)(2,1)}, s32[2,2,1536]{2,1,0:T(2,128)}, bf16[2,512,768]{2,1,0:T(8,128)(2,1)}, f32[2,8,512]{2,1,0:T(8,128)}) custom-call(bf16[2,96,1024]{2,1,0:T(8,128)(2,1)} %tok.5, s32[2,1536]{1,0:T(2,128)} %seg.1, bf16[512,3072]{1,0:T(8,128)(2,1)} %wqkv.1, f32[8,512]{1,0:T(8,128)} %fusion.6.gains), custom_call_target="tpu_custom_call" | custom-call | tf_op jit(solution)/shard_map/open_column/pallas_call | solution.py:426
  38.4 0.0 copy-start.4
  38.4 0.0 copy-start
  38.4 0.9 slice.13
  39.3 1.7 convert_reduce_fusion
  41.0 0.1 div.31
  41.1 2.0 multiply_reduce_fusion
  43.1 0.1 rsqrt.13
  43.2 0.1 fusion.7
  43.4 0.6 broadcast_in_dim.12.seg_row
  44.0 0.9 broadcast_in_dim.14.valid_all
  44.9 1.1 broadcast_in_dim.11.seg_col
  46.1 0.5 multiply_convert_fusion
  46.6 1.7 fusion.2.h_one
  48.3 2.4 convolution_convert_fusion
  50.7 32.0 %to_heads.1 = (bf16[8,192,384]{2,1,0:T(8,128)(2,1)}, bf16[2,512,1024]{2,1,0:T(8,128)(2,1)}) custom-call(bf16[4,192,768]{2,1,0:T(8,128)(2,1)} %bitcast.31, bf16[512,4096]{1,0:T(8,128)(2,1)} %up.1), custom_call_target="tpu_custom_call" | custom-call | tf_op jit(solution)/shard_map/to_heads/pallas_call | solution.py:467
  82.7 12.4 %attend.1 = (bf16[1536,128]{1,0:T(8,128)(2,1)}, f32[1536,128]{1,0:T(8,128)}, f32[1536,128]{1,0:T(8,128)}) custom-call(bf16[1536,384]{1,0:T(8,128)(2,1)} %bitcast.25, s32[1536,128]{1,0:T(8,128)} %broadcast_in_dim.11.seg_col, s32[8,1536]{1,0:T(8,128)} %broadcast_in_dim.12.seg_row), custom_call_target="tpu_custom_call" | custom-call | tf_op jit(solution)/shard_map/attend/pallas_call | solution.py:815
  95.1 67.9 %middle.1 = (bf16[8,192,128]{2,1,0:T(8,128)(2,1)}, bf16[2,96,1024]{2,1,0:T(8,128)(2,1)}, f32[2,96,1024]{2,1,0:T(8,128)}, f32[8,1024]{1,0:T(8,128)}, bf16[9,2,512,256]{3,2,1,0:T(8,128)(2,1)}) custom-call(bf16[8,192,128]{2,1,0:T(8,128)(2,1)} %bitcast.32, bf16[2,96,1024]{2,1,0:T(8,128)(2,1)} %cot.1, bf16[2,96,1024]{2,1,0:T(8,128)(2,1)} %tok.5, ...), custom_call_target="tpu_custom_call" | custom-call | tf_op jit(solution)/shard_map/middle/pallas_call | solution.py:737
  162.9 17.1 %attend_back.1 = bf16[1536,384]{1,0:T(8,128)(2,1)} custom-call(bf16[1536,384]{1,0:T(8,128)(2,1)} %bitcast.26, f32[1536,128]{1,0:T(8,128)} %get-tuple-element.33.out, f32[1536,128]{1,0:T(8,128)} %get-tuple-element.34.lse, bf16[1536,128]{1,0:T(8,128)(2,1)} %bitcast.33, s32[1536,128]{1,0:T(8,128)} %broadcast_in_dim.11.seg_col, s32[8,1536]{1,0:T(8,128)} %broadcast_in_dim.12.seg_row), custom_call_target="tpu_custom_call" | custom-call | tf_op jit(solution)/shard_map/attend_back/pallas_call | solution.py:881
  180.1 163.4 %tail.1 = (f32[2,96,1024]{2,1,0:T(8,128)}, bf16[12,2,2,512,256]{4,3,2,1,0:T(8,128)(2,1)}, f32[8,1024]{1,0:T(8,128)}) custom-call(bf16[8,192,384]{2,1,0:T(8,128)(2,1)} %bitcast.24, bf16[9,2,512,256]{3,2,1,0:T(8,128)(2,1)} %get-tuple-element.36.parts, bf16[1024,768]{1,0:T(8,128)(2,1)} %bitcast.28, bf16[4,192,1024]{2,1,0:T(8,128)(2,1)} %fusion.2.h_one, ...), custom_call_target="tpu_custom_call" | custom-call | tf_op jit(solution)/shard_map/tail/pallas_call | solution.py:1185
  343.4 1.5 fusion.8
  344.9 2.4 widen_out.1
  347.3 5.2 %widen_qkv.1 = f32[512,3072]{1,0:T(8,128)} custom-call(bf16[12,2,2,512,256]{4,3,2,1,0:T(8,128)(2,1)} %get-tuple-element.40.src), custom_call_target="tpu_custom_call" | custom-call | tf_op jit(solution)/shard_map/widen_qkv/pallas_call | solution.py:1262
  352.5 6.0 %widen_down.1 = f32[2048,1024]{1,0:T(8,128)} custom-call(bf16[12,2,2,512,256]{4,3,2,1,0:T(8,128)(2,1)} %get-tuple-element.40.src), custom_call_target="tpu_custom_call" | custom-call | tf_op jit(solution)/shard_map/widen_down/pallas_call | solution.py:1238
  358.5 6.1 %widen_up.1 = f32[512,4096]{1,0:T(8,128)} custom-call(bf16[12,2,2,512,256]{4,3,2,1,0:T(8,128)(2,1)} %get-tuple-element.40.src), custom_call_target="tpu_custom_call" | custom-call | tf_op jit(solution)/shard_map/widen_up/pallas_call | solution.py:1246
  364.6 0.7 copy.19
  365.3 0.9 copy.20
  (12 shorter events, 0.1 us)
Async XLA Ops:
  38.4 4.8 %copy-start.4 = (s32[2,2,1536]{2,1,0:T(2,128)S(1)}, s32[2,2,1536]{2,1,0:T(2,128)}, u32[]{:S(2)}) copy-start(s32[2,2,1536]{2,1,0:T(2,128)} %get-tuple-element.29) | copy-start | bytes 73732
  38.4 7.6 %copy-start = (bf16[4,2,96,1024]{3,2,1,0:T(8,128)(2,1)S(1)}, bf16[4,2,96,1024]{3,2,1,0:T(8,128)(2,1)}, u32[]{:S(2)}) copy-start(bf16[4,2,96,1024]{3,2,1,0:T(8,128)(2,1)} %get-tuple-element.25) | copy-start | bytes 4718596
  46.1 2.2 copy-start.1
  358.5 6.1 %copy-start.3 = (bf16[2,96,1024]{2,1,0:T(8,128)(2,1)S(1)}, bf16[2,96,1024]{2,1,0:T(8,128)(2,1)}, u32[]{:S(2)}) copy-start(bf16[2,96,1024]{2,1,0:T(8,128)(2,1)} %get-tuple-element.52) | copy-start | bytes 1179652
  358.5 6.8 %copy-start.2 = (f32[2,96,1024]{2,1,0:T(8,128)S(1)}, f32[2,96,1024]{2,1,0:T(8,128)}, u32[]{:S(2)}) copy-start(f32[2,96,1024]{2,1,0:T(8,128)} %get-tuple-element.53) | copy-start | bytes 2359300
